TPU v7x, 128 devices: a whole 4x4x4 slice. The times are simulated.
128 devices in a mesh: gy: 32 (over z_hi, x, y), gz: 4 (over z_lo, core).
Axes of the slice: x: 4, y: 4, z: 4 (z_hi: 2, z_lo: 2; z = z_hi * 2 + z_lo), core: 2. Of those that a mesh axis runs over, the one named last changes fastest.
Arguments:
- hessian_one: bfloat16 [6, 256, 256, 256], P(None, 'gy', 'gz'), may hold values from -1 to 1
- hessian_two: bfloat16 [6, 256, 256, 256], P(None, 'gy', 'gz'), may hold values from -0.796875 to 0.796875
- displacement: float32 [3, 256, 256, 256], P(None, 'gy', 'gz'), may hold values from -0.5 to 0.5
Outputs:
- psi_third: float32 [3, 256, 256, 256], P(None, 'gy', 'gz')
- overdensity: float32 [256, 256, 256], P('gy', 'gz')
All inputs are finite; a program needn't handle non-finite values.
Results may differ from a plain program's by a relative error of at most 0.0003.
Values sent between devices are 32-bit elements; how exact they have to be, the bound alone decides.
No kernel may reach another device: no remote copies, remote signals or barrier semaphores. Data moves between devices by JAX's collectives and lax.ppermute only.
A program may use at most 128 MiB of HBM per device.

v0:
```python
import functools

import jax
import jax.numpy as jnp
import numpy as np
from jax import lax
from jax.experimental import pallas as pl
from jax.experimental.pallas import tpu as pltpu
from jax.sharding import PartitionSpec as P

N = 256
HALF = N // 2
ROWS = 8
DEPTH = 64
det_weight = -1.0 / 3.0
mixed_weight = 10.0 / 21.0
f32 = jnp.float32
bf16 = jnp.bfloat16


def split_table(table):
    high = table.astype(np.float32).astype(jnp.bfloat16)
    low = (table - high.astype(np.float64)).astype(np.float32).astype(jnp.bfloat16)
    return np.stack([high, low])


def wave_index():
    order = np.arange(N)
    return np.where(order <= HALF, order, order - HALF)


def real_tables():
    order = np.arange(N)
    wave = wave_index()
    is_sin = order > HALF
    angle = 2.0 * np.pi / N * (wave[:, None] * np.arange(N)[None, :] % N)
    cosine, sine = np.cos(angle), np.sin(angle)
    forward = np.where(is_sin[:, None], sine, cosine)
    single = (order == 0) | (order == HALF)
    weight = np.where(single, 1.0, 2.0)[:, None] / N
    inverse = weight * forward
    number = (2.0 * np.pi / N * np.where(single, 0, wave))[:, None]
    slope = weight * number * np.where(is_sin[:, None], cosine, -sine)
    return forward, inverse, slope


forward_table, inverse_table, slope_table = real_tables()


def split(value):
    high = value.astype(bf16)
    return high, (value - high.astype(f32)).astype(bf16)


def dot3(left, right, dims):
    (left_high, left_low), (right_high, right_low) = left, right
    product = functools.partial(
        lax.dot_general, dimension_numbers=(dims, ((), ())), preferred_element_type=f32
    )
    return product(left_high, right_high) + (
        product(left_high, right_low) + product(left_low, right_high)
    )


NN = ((1,), (0,))
NT = ((1,), (1,))
TN = ((0,), (0,))


def low_lanes(shape):
    return lax.broadcasted_iota(jnp.int32, shape, len(shape) - 1) < DEPTH


def source_term(one, two):
    primary = [one[c].astype(f32) for c in range(6)]
    secondary = [two[c].astype(f32) for c in range(6)]
    determinant = (
        primary[0] * (primary[1] * primary[2] - primary[5] * primary[5])
        - primary[3] * (primary[3] * primary[2] - primary[5] * primary[4])
        + primary[4] * (primary[3] * primary[5] - primary[1] * primary[4])
    )
    mixed = 0.5 * (
        secondary[0] * (primary[1] + primary[2])
        + secondary[1] * (primary[0] + primary[2])
        + secondary[2] * (primary[0] + primary[1])
    )
    mixed = mixed - (
        secondary[3] * primary[3] + secondary[4] * primary[4] + secondary[5] * primary[5]
    )
    return det_weight * determinant + mixed_weight * mixed


def lines_kernel(one_in, two_in, table_in, out_ref, one_ref, two_ref, table_ref, sem):
    table_copy = pltpu.make_async_copy(table_in, table_ref, sem.at[ROWS])
    table_copy.start()
    copies = []
    for pair in range(ROWS // 2):
        rows = slice(2 * pair, 2 * pair + 2)
        for index, (source, target) in enumerate(((one_in, one_ref), (two_in, two_ref))):
            copy = pltpu.make_async_copy(
                source.at[:, rows], target.at[:, rows], sem.at[2 * pair + index]
            )
            copy.start()
            copies.append(copy)
    mask = low_lanes((HALF, 128))
    table_copy.wait()
    for pair in range(ROWS // 2):
        copies[2 * pair].wait()
        copies[2 * pair + 1].wait()
        source = jnp.concatenate(
            [
                source_term(
                    [one_ref[c, row] for c in range(6)], [two_ref[c, row] for c in range(6)]
                )
                for row in (2 * pair, 2 * pair + 1)
            ],
            axis=0,
        )
        result = dot3((table_ref[0], table_ref[1]), split(source), NT)
        first, second = result[:HALF], result[HALF:]
        out_ref[pl.ds(2 * pair, HALF, stride=ROWS), :] = jnp.where(
            mask, first, pltpu.roll(second, DEPTH, 1)
        )
        out_ref[pl.ds(2 * pair + 1, HALF, stride=ROWS), :] = jnp.where(
            mask, pltpu.roll(first, DEPTH, 1), second
        )


def lines(one, two):
    far = pl.BlockSpec(memory_space=pltpu.HBM)
    return pl.pallas_call(
        lines_kernel,
        in_specs=[far] * 3,
        out_specs=pl.BlockSpec(memory_space=pltpu.VMEM),
        out_shape=jax.ShapeDtypeStruct((HALF * ROWS, 128), f32),
        scratch_shapes=[
            pltpu.VMEM((6, ROWS, DEPTH, N), bf16),
            pltpu.VMEM((6, ROWS, DEPTH, N), bf16),
            pltpu.VMEM((2, N, N), bf16),
            pltpu.SemaphoreType.DMA((ROWS + 1,)),
        ],
        compiler_params=pltpu.CompilerParams(vmem_limit_bytes=60 << 20),
        name="lines",
    )(one, two, jnp.asarray(split_table(forward_table)))


def planes_kernel(in_ref, forward_ref, inverse_ref, slope_ref, inverse_t_ref, slope_t_ref, out_ref):
    mask = low_lanes((N, 128))
    tiles = [in_ref[:, g].reshape(N, 128) for g in range(4)]
    swapped = [pltpu.roll(tile, DEPTH, 1) for tile in tiles]
    first = [jnp.where(mask, tiles[g], swapped[g + 1]) for g in (0, 2)]
    second = [jnp.where(mask, swapped[g], tiles[g + 1]) for g in (0, 2)]
    stacked = jnp.concatenate(
        [jnp.concatenate(first, axis=1), jnp.concatenate(second, axis=1)], axis=0
    )
    forward = (forward_ref[0], forward_ref[1])
    inverse = (inverse_ref[0], inverse_ref[1])
    slope = (slope_ref[0], slope_ref[1])
    inverse_t = (inverse_t_ref[0], inverse_t_ref[1])
    slope_t = (slope_t_ref[0], slope_t_ref[1])
    depth = dot3(split(stacked), forward, NT)
    step = 2.0 * np.pi / N
    rows = lax.broadcasted_iota(jnp.int32, (N, N), 0)
    columns = lax.broadcasted_iota(jnp.int32, (N, N), 1)
    wave_rows = jnp.where(rows > HALF, rows - HALF, rows).astype(f32) * step
    wave_columns = jnp.where(columns > HALF, columns - HALF, columns).astype(f32) * step
    plane_square = wave_rows * wave_rows + wave_columns * wave_columns
    first_line = lax.axis_index("gy") * lax.axis_size("gz") + lax.axis_index("gz")
    filtered = []
    for part in range(2):
        spectrum = dot3(forward, split(depth[part * N : (part + 1) * N]), NN)
        line = first_line + (HALF if part == 1 else 0) * (first_line == 0).astype(jnp.int32)
        wave_line = line.astype(f32) * step
        square = plane_square + wave_line * wave_line
        filtered.append(
            jnp.where(square > 0.0, spectrum / jnp.where(square > 0.0, square, 1.0), 0.0)
        )
    stacked = split(jnp.concatenate(filtered, axis=0))
    plain = split(dot3(stacked, inverse, NN))
    sloped = split(dot3(stacked, slope, NN))
    part_of = lambda pair, part: tuple(v[part * N : (part + 1) * N] for v in pair)
    for field, (matrix, values) in enumerate(
        ((inverse_t, plain), (slope_t, plain), (inverse_t, sloped))
    ):
        first = dot3(matrix, part_of(values, 0), NN)
        second = dot3(matrix, part_of(values, 1), NN)
        for g in (0, 2):
            lanes = slice(g * DEPTH, g * DEPTH + 128)
            a, b = first[:, lanes], second[:, lanes]
            even = jnp.where(mask, a, pltpu.roll(b, DEPTH, 1))
            odd = jnp.where(mask, pltpu.roll(a, DEPTH, 1), b)
            out_ref[:, g, field * ROWS : (field + 1) * ROWS, :] = even.reshape(32, ROWS, 128)
            out_ref[:, g + 1, field * ROWS : (field + 1) * ROWS, :] = odd.reshape(32, ROWS, 128)


def planes(values):
    whole = pl.BlockSpec(memory_space=pltpu.VMEM)
    tables = [
        jnp.asarray(split_table(t))
        for t in (forward_table, inverse_table, slope_table, inverse_table.T, slope_table.T)
    ]
    return pl.pallas_call(
        planes_kernel,
        in_specs=[whole] * 6,
        out_specs=whole,
        out_shape=jax.ShapeDtypeStruct((32, 4, 3 * ROWS, 128), f32),
        compiler_params=pltpu.CompilerParams(vmem_limit_bytes=24 << 20),
        name="planes",
    )(values, *tables)


PAD = 8
HELD = DEPTH + 3 * PAD
EDGE_ROWS = (0, 1, ROWS - 2, ROWS - 1)
EVERY_ROW = tuple(range(ROWS))


def tile_weights(moved):
    weights = []
    for shift in range(5):
        offset = moved + (shift - 2.0) if shift != 2 else moved
        outer = jnp.maximum(2.0 - jnp.abs(offset), 0.0)
        weights.append(
            jnp.minimum(4.0 - 3.0 * ((offset * offset) * outer), (outer * outer) * outer)
        )
    return weights


def row_pair(row, slots, in_ref, displacement_ref, inverse, slope, psi_ref, weight_ref):
    mask = low_lanes((HALF, 128))
    for slot in slots:
        zeros = jnp.zeros((15, 2, PAD, 128), f32)
        weight_ref[slot, :, :, 0:PAD, :] = zeros
        weight_ref[slot, :, :, PAD + DEPTH : 2 * PAD + DEPTH, :] = zeros
    for field in range(3):
        start = field * ROWS + row
        even = in_ref[pl.ds(start, HALF, stride=3 * ROWS), :]
        odd = in_ref[pl.ds(start + 1, HALF, stride=3 * ROWS), :]
        first = jnp.where(mask, even, pltpu.roll(odd, DEPTH, 1))
        second = jnp.where(mask, pltpu.roll(even, DEPTH, 1), odd)
        stacked = jnp.concatenate([first, second], axis=0)
        result = dot3(split(stacked), slope if field == 0 else inverse, TN)
        for part, slot in enumerate(slots):
            values = result[part * DEPTH : (part + 1) * DEPTH]
            psi_ref[slot, field] = values
            for tile in range(DEPTH // 8):
                for half in range(2):
                    lanes = slice(half * 128, half * 128 + 128)
                    rows = slice(tile * 8, tile * 8 + 8)
                    moved = displacement_ref[field, row + part, rows, lanes] + values[rows, lanes]
                    for shift, weight in enumerate(tile_weights(moved)):
                        place = slice(PAD + tile * 8, PAD + tile * 8 + 8)
                        weight_ref[slot, 5 * field + shift, half, place, :] = weight
                        if tile == 0:
                            weight_ref[slot, 5 * field + shift, half, HELD - PAD : HELD, :] = weight


def line_sums(carry_ref):
    lane = lax.broadcasted_iota(jnp.int32, (8, 128), 1)
    low, high = carry_ref[0, 2], carry_ref[1, 2]
    for shift_line in (0, 1, 3, 4):
        move = 2 - shift_line
        a = pltpu.roll(carry_ref[0, shift_line], move % 128, 1)
        b = pltpu.roll(carry_ref[1, shift_line], move % 128, 1)
        wraps = lane < move if move > 0 else lane >= 128 + move
        low = low + jnp.where(wraps, b, a)
        high = high + jnp.where(wraps, a, b)
    return low * (1.0 / 216.0), high * (1.0 / 216.0)


def collect(carry_ref, pairs, out_ref, row):
    def store(start):
        low, high = line_sums(carry_ref)
        out_ref[row, pl.ds(start, 8), 0:128] = low
        out_ref[row, pl.ds(start, 8), 128:256] = high

    @pl.loop(0, DEPTH // 8 + 1)
    def _(tile):
        start = pl.multiple_of(tile * 8, 8)
        store(pl.multiple_of(jnp.maximum(tile - 1, 0) * 8, 8))
        for half in range(2):
            totals = None
            for (weight_ref, slot), shift_row in pairs:
                terms = []
                for shift_depth in range(5):
                    where = pl.ds(start + PAD - 2 + shift_depth, 8)
                    get = lambda index: weight_ref[slot, index, half, where, :]
                    plane = get(5 + shift_row) * get(10 + shift_depth)
                    terms.append([plane * get(s) for s in range(5)])
                sums = [(a + b) + (c + d) + e for a, b, c, d, e in zip(*terms)]
                totals = sums if totals is None else [a + b for a, b in zip(totals, sums)]
            for shift_line in range(5):
                carry_ref[half, shift_line] = totals[shift_line]

    store(DEPTH)


def reach(cell, held):
    return [(held[row], row + 2 - cell) for row in sorted(held) if 0 <= row + 2 - cell < 5]


def edges_kernel(
    in_ref, displacement_ref, inverse_ref, slope_ref,
    psi_out, weight_ref, first_ref, second_ref,
    psi_ref, carry_ref, psi_sem,
):
    inverse = (inverse_ref[0], inverse_ref[1])
    slope = (slope_ref[0], slope_ref[1])
    copies = []
    for pair, row in enumerate((0, ROWS - 2)):
        slots = (2 * pair, 2 * pair + 1)
        row_pair(row, slots, in_ref, displacement_ref, inverse, slope, psi_ref, weight_ref)
        for part, slot in enumerate(slots):
            copy = pltpu.make_async_copy(
                psi_ref.at[slot], psi_out.at[:, row + part], psi_sem.at[slot]
            )
            copy.start()
            copies.append(copy)
    held = {row: (weight_ref, slot) for slot, row in enumerate(EDGE_ROWS)}

    def cells(before_ref, after_ref):
        for index in range(2):
            collect(carry_ref, reach(index - 2, held), before_ref, index)
            collect(carry_ref, reach(ROWS + index, held), after_ref, index)

    odd = lax.axis_index("gy") % 2

    @pl.when(odd == 0)
    def _():
        cells(second_ref, first_ref)

    @pl.when(odd != 0)
    def _():
        cells(first_ref, second_ref)

    for copy in copies:
        copy.wait()


VMEM = pl.BlockSpec(memory_space=pltpu.VMEM)
SMEM = pl.BlockSpec(memory_space=pltpu.SMEM)
ANY = pl.BlockSpec(memory_space=pl.ANY)


def edges(values, displacement, tables):
    halo = jax.ShapeDtypeStruct((2, DEPTH + PAD, N), f32)
    return pl.pallas_call(
        edges_kernel,
        in_specs=[VMEM] * 4,
        out_specs=[ANY, VMEM, VMEM, VMEM],
        out_shape=[
            jax.ShapeDtypeStruct((3, ROWS, DEPTH, N), f32),
            jax.ShapeDtypeStruct((4, 15, 2, HELD, 128), f32),
            halo,
            halo,
        ],
        scratch_shapes=[
            pltpu.VMEM((4, 3, DEPTH, N), f32),
            pltpu.VMEM((2, 5, 8, 128), f32),
            pltpu.SemaphoreType.DMA((4,)),
        ],
        compiler_params=pltpu.CompilerParams(vmem_limit_bytes=16 << 20),
        name="edges",
    )(values, displacement, *tables)


def inner_kernel(
    in_ref, displacement_ref, inverse_ref, slope_ref, psi_in, edge_ref,
    psi_out, out_ref,
    psi_ref, weight_ref, carry_ref, psi_sem,
):
    inverse = (inverse_ref[0], inverse_ref[1])
    slope = (slope_ref[0], slope_ref[1])
    copies = []
    for row in (2, 4):
        slots = (row - 2, row - 1)
        row_pair(row, slots, in_ref, displacement_ref, inverse, slope, psi_ref, weight_ref)
        for slot in slots:
            copy = pltpu.make_async_copy(
                psi_ref.at[slot], psi_out.at[:, slot + 2], psi_sem.at[slot]
            )
            copy.start()
            copies.append(copy)
    held = {row: (edge_ref, slot) for slot, row in enumerate(EDGE_ROWS)}
    held.update({row: (weight_ref, row - 2) for row in range(2, ROWS - 2)})
    for row in range(ROWS):
        collect(carry_ref, reach(row, held), out_ref, row)
    for copy in copies:
        copy.wait()


def inner(values, displacement, tables, psi, weights):
    return pl.pallas_call(
        inner_kernel,
        in_specs=[VMEM] * 4 + [ANY, VMEM],
        out_specs=[ANY, VMEM],
        out_shape=[
            jax.ShapeDtypeStruct((3, ROWS, DEPTH, N), f32),
            jax.ShapeDtypeStruct((ROWS, DEPTH + PAD, N), f32),
        ],
        scratch_shapes=[
            pltpu.VMEM((4, 3, DEPTH, N), f32),
            pltpu.VMEM((4, 15, 2, HELD, 128), f32),
            pltpu.VMEM((2, 5, 8, 128), f32),
            pltpu.SemaphoreType.DMA((4,)),
        ],
        input_output_aliases={4: 0},
        compiler_params=pltpu.CompilerParams(vmem_limit_bytes=20 << 20),
        name="inner",
    )(values, displacement, *tables, psi, weights)


def halos(first_ref, second_ref, where):
    even = lax.axis_index("gy") % 2 == 0
    first, second = first_ref[:, where, :], second_ref[:, where, :]
    return jnp.where(even, second, first), jnp.where(even, first, second)


def sides_kernel(cell_ref, first_ref, second_ref, out_ref):
    low, high = halos(first_ref, second_ref, slice(None))
    side = cell_ref[...]
    out_ref[0:2] = side[0:2] + low
    out_ref[2 : ROWS - 2] = side[2 : ROWS - 2]
    out_ref[ROWS - 2 :] = side[ROWS - 2 :] + high


def sides(cells, first, second):
    last = DEPTH // PAD
    block = lambda rows: pl.BlockSpec((rows, PAD, N), lambda i: (0, last, 0))
    return pl.pallas_call(
        sides_kernel,
        grid=(1,),
        in_specs=[block(ROWS), block(2), block(2)],
        out_specs=pl.BlockSpec((ROWS, PAD, N), lambda i: (0, 0, 0)),
        out_shape=jax.ShapeDtypeStruct((ROWS, PAD, N), f32),
        compiler_params=pltpu.CompilerParams(vmem_limit_bytes=8 << 20),
        name="sides",
    )(cells, first, second)


def sum_kernel(cell_ref, first_ref, second_ref, left_ref, right_ref, out_ref):
    low, high = halos(first_ref, second_ref, slice(0, DEPTH))
    sub = lax.broadcasted_iota(jnp.int32, (PAD, N), 0)
    for row in range(ROWS):
        value = cell_ref[row, :DEPTH, :] - 1.0
        if row < 2:
            value = value + low[row]
        if row >= ROWS - 2:
            value = value + high[row - ROWS + 2]
        out_ref[row, 0:8, :] = value[0:8] + jnp.where(sub < 2, left_ref[row], 0.0)
        out_ref[row, 8:56, :] = value[8:56]
        out_ref[row, 56:64, :] = value[56:64] + jnp.where(sub >= 6, right_ref[row], 0.0)


def total(*parts):
    return pl.pallas_call(
        sum_kernel,
        in_specs=[VMEM] * 5,
        out_specs=VMEM,
        out_shape=jax.ShapeDtypeStruct((ROWS, DEPTH, N), f32),
        compiler_params=pltpu.CompilerParams(vmem_limit_bytes=8 << 20),
        name="total",
    )(*parts)


def local(hessian_one, hessian_two, displacement):
    size_y, size_z = lax.axis_size("gy"), lax.axis_size("gz")
    both = ("gy", "gz")
    spectra = lines(hessian_one, hessian_two).reshape(HALF, ROWS, 128)
    spectra = lax.all_to_all(spectra, both, split_axis=0, concat_axis=0, tiled=True)
    returned = planes(spectra.reshape(32, 4, ROWS, 128))
    returned = returned.reshape(HALF, 3 * ROWS, 128)
    returned = lax.all_to_all(returned, both, split_axis=0, concat_axis=0, tiled=True)
    returned = returned.reshape(HALF * 3 * ROWS, 128)
    tables = [jnp.asarray(split_table(t)) for t in (inverse_table, slope_table)]
    psi, weights, first, second = edges(returned, displacement, tables)
    first = lax.ppermute(first, "gy", [(i, i ^ 1) for i in range(size_y)])
    second = lax.ppermute(
        second, "gy", [(i, (i + (1 if i % 2 else -1)) % size_y) for i in range(size_y)]
    )
    psi, cells = inner(returned, displacement, tables, psi, weights)
    side = sides(cells, first, second)
    up = [(i, (i + 1) % size_z) for i in range(size_z)]
    down = [(j, i) for i, j in up]
    left = lax.ppermute(side, "gz", up)
    right = lax.ppermute(side, "gz", down)
    density = total(cells, first, second, left, right)
    return psi, density


def solution(mesh):
    in_specs = (P(None, "gy", "gz", None), P(None, "gy", "gz", None), P(None, "gy", "gz", None))
    out_specs = (P(None, "gy", "gz", None), P("gy", "gz", None))
    return jax.shard_map(local, mesh=mesh, in_specs=in_specs, out_specs=out_specs, check_vma=False)
```

profile of v0, /device:TPU:1, one launch (start us, length us, event | category | flops | bytes accessed | tf_op | source)
XLA Modules:
  0.0 84.8 jit_solution(5174334340786293783)
XLA Ops:
  0.6 0.0 copy-start.1
  0.6 0.0 copy-start.2
  0.7 0.0 copy-start.3
  0.7 0.0 copy-start.4
  0.7 0.0 copy-start.5
  0.7 4.5 %lines.1 = f32[1024,128]{1,0:T(8,128)} custom-call(bf16[6,8,64,256]{3,2,1,0:T(8,128)(2,1)} %one_in.1, bf16[6,8,64,256]{3,2,1,0:T(8,128)(2,1)} %two_in.1, bf16[2,256,256]{2,1,0:T(8,128)(2,1)} %constant.10.clone.table_in.forward_ref), custom_call_target="tpu_custom_call" | custom-call | tf_op jit(solution)/shard_map/lines/pallas_call | solution.py:131
  5.2 25.1 %all_to_all.10 = f32[128,8,128]{2,1,0:T(8,128)S(1)} all-to-all(f32[128,8,128]{2,1,0:T(8,128)} %bitcast.8), channel_id=1, replica_groups=mesh['gy'=32,'gz'=4] {'gy','gz'}, dimensions={0} | all-to-all | bytes 1048576 | tf_op jit(solution)/shard_map/all_to_all | solution.py:470
  30.3 0.0 copy-done.1
  30.3 0.0 copy-done.2
  30.3 0.0 copy-done.3
  30.3 0.0 copy-done.4
  30.3 0.0 copy-done.5
  30.3 2.3 %planes.1 = f32[32,4,24,128]{3,2,1,0:T(8,128)S(1)} custom-call(f32[32,4,8,128]{3,2,1,0:T(8,128)S(1)} %bitcast.7, bf16[2,256,256]{2,1,0:T(8,128)(2,1)S(1)} %copy-done.3, bf16[2,256,256]{2,1,0:T(8,128)(2,1)S(1)} %copy-done.2, bf16[2,256,256]{2,1,0:T(8,128)(2,1)S(1)} %copy-done.1, bf16[2,256,256]{2,1,0:T(8,128)(2,1)S(1)} %copy-done.5, ...), custom_call_target="tpu_custom_call" | custom-call | tf_op jit(solution)/shard_map/planes/pallas_call | solution.py:202
  32.6 0.0 copy-start
  32.6 28.7 %all_to_all.11 = f32[128,24,128]{2,1,0:T(8,128)S(1)} all-to-all(f32[128,24,128]{2,1,0:T(8,128)S(1)} %bitcast.6), channel_id=1, replica_groups=mesh['gy'=32,'gz'=4] {'gy','gz'}, dimensions={0} | all-to-all | bytes 3145728 | tf_op jit(solution)/shard_map/all_to_all | solution.py:473
  61.3 0.0 copy-done
  61.3 5.0 %edges.1 = (f32[3,8,64,256]{3,2,1,0:T(8,128)}, f32[4,15,2,88,128]{4,3,2,1,0:T(8,128)S(1)}, f32[2,72,256]{2,1,0:T(8,128)S(1)}, f32[2,72,256]{2,1,0:T(8,128)S(1)}) custom-call(f32[3072,128]{1,0:T(8,128)S(1)} %bitcast.4, f32[3,8,64,256]{3,2,1,0:T(8,128)S(1)} %copy-done, bf16[2,256,256]{2,1,0:T(8,128)(2,1)S(1)} %copy-done.2, bf16[2,256,256]{2,1,0:T(8,128)(2,1)S(1)} %copy-done.1), custom_call_target="tpu_custom_call" | custom-call | tf_op jit(solution)/shard_map/edges/pallas_call | solution.py:347
  66.3 1.4 %collective-permute-start = (f32[2,72,256]{2,1,0:T(8,128)S(1)}, f32[2,72,256]{2,1,0:T(8,128)S(1)}, u32[]{:S(2)}, u32[]{:S(2)}) collective-permute-start(f32[2,72,256]{2,1,0:T(8,128)S(1)} %get-tuple-element.12), channel_id=1, source_target_pairs={{0,4},{4,0},{8,12},{12,8},{16,20},{20,16},{24,28},{28,24},{32,36},... | collective-permute-start | bytes 442376 | tf_op jit(solution)/shard_map/ppermute | solution.py:477
  67.7 1.8 %collective-permute-start.1 = (f32[2,72,256]{2,1,0:T(8,128)S(1)}, f32[2,72,256]{2,1,0:T(8,128)S(1)}, u32[]{:S(2)}, u32[]{:S(2)}) collective-permute-start(f32[2,72,256]{2,1,0:T(8,128)S(1)} %get-tuple-element.13), channel_id=1, source_target_pairs={{0,124},{4,8},{8,4},{12,16},{16,12},{20,24},{24,20},{28,32},{32,28... | collective-permute-start | bytes 442376 | tf_op jit(solution)/shard_map/ppermute | solution.py:478
  69.5 10.1 %inner.1 = (f32[3,8,64,256]{3,2,1,0:T(8,128)}, f32[8,72,256]{2,1,0:T(8,128)S(1)}) custom-call(f32[3072,128]{1,0:T(8,128)S(1)} %bitcast.5, f32[3,8,64,256]{3,2,1,0:T(8,128)S(1)} %copy-done, bf16[2,256,256]{2,1,0:T(8,128)(2,1)S(1)} %copy-done.2, bf16[2,256,256]{2,1,0:T(8,128)(2,1)S(1)} %copy-done.1, ...), custom_call_target="tpu_custom_call", output_to_operand_aliasing={{0}: (4, {})} | custom-call | tf_op jit(solution)/shard_map/inner/pallas_call | solution.py:393
  79.6 0.0 collective-permute-done.first_ref
  79.6 0.0 collective-permute-done.1.second_ref
  79.7 1.2 %collective-permute-start.3 = (f32[8,8,256]{2,1,0:T(8,128)S(1)}, f32[8,8,256]{2,1,0:T(8,128)S(1)}, u32[]{:S(2)}, u32[]{:S(2)}) collective-permute-start(f32[8,8,256]{2,1,0:T(8,128)S(1)} %sides.1), channel_id=1, source_target_pairs={{1,0},{2,1},{3,2},{0,3},{5,4},{6,5},{7,6},{4,7},{9,8},{10,9},{11,1... | collective-permute-start | bytes 196616 | tf_op jit(solution)/shard_map/ppermute | solution.py:486
  80.9 0.6 collective-permute-start.2
  81.5 2.4 %collective-permute-done.3.right_ref = f32[8,8,256]{2,1,0:T(8,128)S(1)} collective-permute-done((f32[8,8,256]{2,1,0:T(8,128)S(1)}, f32[8,8,256]{2,1,0:T(8,128)S(1)}, u32[]{:S(2)}, u32[]{:S(2)}) %collective-permute-start.3) | collective-permute-done | bytes 65568 | tf_op jit(solution)/shard_map/ppermute | solution.py:486
  83.9 0.0 collective-permute-done.2.left_ref
  83.9 0.9 %total.1 = f32[8,64,256]{2,1,0:T(8,128)} custom-call(f32[8,72,256]{2,1,0:T(8,128)S(1)} %get-tuple-element.11.cell_ref, f32[2,72,256]{2,1,0:T(8,128)S(1)} %collective-permute-done.first_ref, f32[2,72,256]{2,1,0:T(8,128)S(1)} %collective-permute-done.1.second_ref, f32[8,8,256]{2,1,0:T(8,128)S(1)} %collective-permute-done.2.left_ref, ...), custom_call_target="tpu_custom_call" | custom-call | tf_op jit(solution)/shard_map/total/pallas_call | solution.py:456
  (1 shorter events, 0.0 us)
Async XLA Ops:
  0.6 29.6 %copy-start.1 = (bf16[2,256,256]{2,1,0:T(8,128)(2,1)S(1)}, bf16[2,256,256]{2,1,0:T(8,128)(2,1)}, u32[]{:S(2)}) copy-start(bf16[2,256,256]{2,1,0:T(8,128)(2,1)} %constant.12.clone.slope_ref) | copy-start | bytes 786436
  0.6 29.6 %copy-start.2 = (bf16[2,256,256]{2,1,0:T(8,128)(2,1)S(1)}, bf16[2,256,256]{2,1,0:T(8,128)(2,1)}, u32[]{:S(2)}) copy-start(bf16[2,256,256]{2,1,0:T(8,128)(2,1)} %constant.11.clone.inverse_ref) | copy-start | bytes 786436
  0.7 29.6 %copy-start.3 = (bf16[2,256,256]{2,1,0:T(8,128)(2,1)S(1)}, bf16[2,256,256]{2,1,0:T(8,128)(2,1)}, u32[]{:S(2)}) copy-start(bf16[2,256,256]{2,1,0:T(8,128)(2,1)} %constant.10.clone.table_in.forward_ref) | copy-start | bytes 786436
  0.7 29.6 %copy-start.4 = (bf16[2,256,256]{2,1,0:T(8,128)(2,1)S(1)}, bf16[2,256,256]{2,1,0:T(8,128)(2,1)}, u32[]{:S(2)}) copy-start(bf16[2,256,256]{2,1,0:T(8,128)(2,1)} %constant.14.clone.slope_t_ref) | copy-start | bytes 786436
  0.7 29.6 %copy-start.5 = (bf16[2,256,256]{2,1,0:T(8,128)(2,1)S(1)}, bf16[2,256,256]{2,1,0:T(8,128)(2,1)}, u32[]{:S(2)}) copy-start(bf16[2,256,256]{2,1,0:T(8,128)(2,1)} %constant.13.clone.inverse_t_ref) | copy-start | bytes 786436
  32.6 28.7 %copy-start = (f32[3,8,64,256]{3,2,1,0:T(8,128)S(1)}, f32[3,8,64,256]{3,2,1,0:T(8,128)}, u32[]{:S(2)}) copy-start(f32[3,8,64,256]{3,2,1,0:T(8,128)} %displacement_ref.3) | copy-start | bytes 4718596
  66.3 13.3 %collective-permute-start = (f32[2,72,256]{2,1,0:T(8,128)S(1)}, f32[2,72,256]{2,1,0:T(8,128)S(1)}, u32[]{:S(2)}, u32[]{:S(2)}) collective-permute-start(f32[2,72,256]{2,1,0:T(8,128)S(1)} %get-tuple-element.12), channel_id=1, source_target_pairs={{0,4},{4,0},{8,12},{12,8},{16,20},{20,16},{24,28},{28,24},{32,36},... | collective-permute-start | bytes 442376 | tf_op jit(solution)/shard_map/ppermute | solution.py:477
  67.7 11.9 %collective-permute-start.1 = (f32[2,72,256]{2,1,0:T(8,128)S(1)}, f32[2,72,256]{2,1,0:T(8,128)S(1)}, u32[]{:S(2)}, u32[]{:S(2)}) collective-permute-start(f32[2,72,256]{2,1,0:T(8,128)S(1)} %get-tuple-element.13), channel_id=1, source_target_pairs={{0,124},{4,8},{8,4},{12,16},{16,12},{20,24},{24,20},{28,32},{32,28... | collective-permute-start | bytes 442376 | tf_op jit(solution)/shard_map/ppermute | solution.py:478
  79.7 4.2 %collective-permute-start.3 = (f32[8,8,256]{2,1,0:T(8,128)S(1)}, f32[8,8,256]{2,1,0:T(8,128)S(1)}, u32[]{:S(2)}, u32[]{:S(2)}) collective-permute-start(f32[8,8,256]{2,1,0:T(8,128)S(1)} %sides.1), channel_id=1, source_target_pairs={{1,0},{2,1},{3,2},{0,3},{5,4},{6,5},{7,6},{4,7},{9,8},{10,9},{11,1... | collective-permute-start | bytes 196616 | tf_op jit(solution)/shard_map/ppermute | solution.py:486
  80.9 3.0 %collective-permute-start.2 = (f32[8,8,256]{2,1,0:T(8,128)S(1)}, f32[8,8,256]{2,1,0:T(8,128)S(1)}, u32[]{:S(2)}, u32[]{:S(2)}) collective-permute-start(f32[8,8,256]{2,1,0:T(8,128)S(1)} %sides.1), channel_id=1, source_target_pairs={{0,1},{1,2},{2,3},{3,0},{4,5},{5,6},{6,7},{7,4},{8,9},{9,10},{10,1... | collective-permute-start | bytes 196616 | tf_op jit(solution)/shard_map/ppermute | solution.py:485
where the time goes:
time: 85 us; the launch traced here: 84.8 us
  blocking collectives  53.8 us (63%)
  Pallas kernels  22.8 us (27%)
  starting transfers between devices  5.02 us (6%)
  waiting for transfers between devices  2.41 us (3%)
    all_to_all x1, blocking collectives, local(): lax.all_to_all(returned, both, split_axis=0, concat_axis=0, tiled=True)  28.7 us
    all_to_all x1, blocking collectives, local(): lax.all_to_all(spectra, both, split_axis=0, concat_axis=0, tiled=True)  25.1 us
    pallas_call x1, Pallas kernels, inner(): pl.pallas_call(inner_kernel, in_specs=[VMEM] * 4 + [ANY, VMEM], out_specs...  10.1 us
    pallas_call x1, Pallas kernels, edges(): pl.pallas_call(edges_kernel, in_specs=[VMEM] * 4, out_specs=[ANY, VMEM, V...  5.01 us
    pallas_call x1, Pallas kernels, lines(): pl.pallas_call(lines_kernel, in_specs=[far] * 3, out_specs=pl.BlockSpec(m...  4.5 us
    ppermute x1, waiting for transfers between devices, local(): right = lax.ppermute(side, 'gz', down)  2.4 us
    pallas_call x1, Pallas kernels, planes(): pl.pallas_call(planes_kernel, in_specs=[whole] * 6, out_specs=whole, out_...  2.27 us
    ppermute x1, starting transfers between devices, local(): lax.ppermute(second, 'gy', [(i, (i + (1 if i % 2 else -1)) % size_y) for...  1.82 us
  transfers between devices with their start and end apart: 4, of which 1 were waited for; matrix products, arithmetic and copies ran while one was open for 0% of the time, Pallas kernels for 12%

commit v1 on v0

--- a/solution.py
+++ b/solution.py
@@ -139,7 +139,7 @@
             pltpu.VMEM((2, N, N), bf16),
             pltpu.SemaphoreType.DMA((ROWS + 1,)),
         ],
-        compiler_params=pltpu.CompilerParams(vmem_limit_bytes=60 << 20),
+        compiler_params=pltpu.CompilerParams(vmem_limit_bytes=61 << 20),
         name="lines",
     )(one, two, jnp.asarray(split_table(forward_table)))
 
@@ -210,7 +210,7 @@
 
 
 PAD = 8
-HELD = DEPTH + 3 * PAD
+HELD = DEPTH + 2 * PAD
 EDGE_ROWS = (0, 1, ROWS - 2, ROWS - 1)
 EVERY_ROW = tuple(range(ROWS))
 
@@ -228,10 +228,6 @@
 
 def row_pair(row, slots, in_ref, displacement_ref, inverse, slope, psi_ref, weight_ref):
     mask = low_lanes((HALF, 128))
-    for slot in slots:
-        zeros = jnp.zeros((15, 2, PAD, 128), f32)
-        weight_ref[slot, :, :, 0:PAD, :] = zeros
-        weight_ref[slot, :, :, PAD + DEPTH : 2 * PAD + DEPTH, :] = zeros
     for field in range(3):
         start = field * ROWS + row
         even = in_ref[pl.ds(start, HALF, stride=3 * ROWS), :]
@@ -249,50 +245,75 @@
                     rows = slice(tile * 8, tile * 8 + 8)
                     moved = displacement_ref[field, row + part, rows, lanes] + values[rows, lanes]
                     for shift, weight in enumerate(tile_weights(moved)):
-                        place = slice(PAD + tile * 8, PAD + tile * 8 + 8)
-                        weight_ref[slot, 5 * field + shift, half, place, :] = weight
-                        if tile == 0:
-                            weight_ref[slot, 5 * field + shift, half, HELD - PAD : HELD, :] = weight
-
-
-def line_sums(carry_ref):
+                        weight_ref[slot, 5 * field + shift, half, rows, :] = weight
+
+
+def shift_lines(halves):
     lane = lax.broadcasted_iota(jnp.int32, (8, 128), 1)
-    low, high = carry_ref[0, 2], carry_ref[1, 2]
+    low, high = halves[0][2], halves[1][2]
     for shift_line in (0, 1, 3, 4):
         move = 2 - shift_line
-        a = pltpu.roll(carry_ref[0, shift_line], move % 128, 1)
-        b = pltpu.roll(carry_ref[1, shift_line], move % 128, 1)
+        a = pltpu.roll(halves[0][shift_line], move % 128, 1)
+        b = pltpu.roll(halves[1][shift_line], move % 128, 1)
         wraps = lane < move if move > 0 else lane >= 128 + move
         low = low + jnp.where(wraps, b, a)
         high = high + jnp.where(wraps, a, b)
     return low * (1.0 / 216.0), high * (1.0 / 216.0)
 
 
-def collect(carry_ref, pairs, out_ref, row):
-    def store(start):
-        low, high = line_sums(carry_ref)
-        out_ref[row, pl.ds(start, 8), 0:128] = low
-        out_ref[row, pl.ds(start, 8), 128:256] = high
-
-    @pl.loop(0, DEPTH // 8 + 1)
-    def _(tile):
-        start = pl.multiple_of(tile * 8, 8)
-        store(pl.multiple_of(jnp.maximum(tile - 1, 0) * 8, 8))
-        for half in range(2):
-            totals = None
-            for (weight_ref, slot), shift_row in pairs:
-                terms = []
-                for shift_depth in range(5):
-                    where = pl.ds(start + PAD - 2 + shift_depth, 8)
-                    get = lambda index: weight_ref[slot, index, half, where, :]
-                    plane = get(5 + shift_row) * get(10 + shift_depth)
-                    terms.append([plane * get(s) for s in range(5)])
-                sums = [(a + b) + (c + d) + e for a, b, c, d, e in zip(*terms)]
-                totals = sums if totals is None else [a + b for a, b in zip(totals, sums)]
+def add_up(terms):
+    while len(terms) > 1:
+        terms = [sum(terms[i : i + 2][1:], terms[i]) for i in range(0, len(terms), 2)]
+    return terms[0]
+
+
+def collect(sum_ref, jobs):
+    for half in range(2):
+        for shift_depth in range(5):
             for shift_line in range(5):
-                carry_ref[half, shift_line] = totals[shift_line]
-
-    store(DEPTH)
+                zeros = jnp.zeros((PAD, 128), f32)
+                sum_ref[half, shift_depth, shift_line, 0:PAD, :] = zeros
+                sum_ref[half, shift_depth, shift_line, HELD - PAD : HELD, :] = zeros
+
+    for pairs, out_ref, row in jobs:
+
+        @pl.loop(0, DEPTH // 8)
+        def _(tile):
+            start = pl.multiple_of(tile * 8, 8)
+            for half in range(2):
+                totals = None
+                for (weight_ref, slot), shift_row in pairs:
+                    get = lambda i: weight_ref[slot, i, half, pl.ds(start, 8), :]
+                    line_weights = [get(i) for i in range(5)]
+                    row_weight = get(5 + shift_row)
+                    planes = [row_weight * get(10 + d) for d in range(5)]
+                    terms = [[plane * w for w in line_weights] for plane in planes]
+                    totals = (
+                        terms
+                        if totals is None
+                        else [[a + b for a, b in zip(x, y)] for x, y in zip(totals, terms)]
+                    )
+                for d in range(5):
+                    for shift_line in range(5):
+                        value = totals[d][shift_line]
+                        sum_ref[half, d, shift_line, pl.ds(start + PAD, 8), :] = value
+
+        for tile in range(DEPTH // 8 + 1):
+            if tile < DEPTH // 8:
+                places = [(d, tile * 8 + PAD - 2 + d) for d in range(5)]
+            else:
+                places = [(d, PAD + DEPTH - 2 + d) for d in (0, 1)]
+                places += [(d, d - 2) for d in (3, 4)]
+            halves = [
+                [
+                    add_up([sum_ref[half, d, shift_line, at : at + 8, :] for d, at in places])
+                    for shift_line in range(5)
+                ]
+                for half in range(2)
+            ]
+            low, high = shift_lines(halves)
+            out_ref[row, tile * 8 : tile * 8 + 8, 0:128] = low
+            out_ref[row, tile * 8 : tile * 8 + 8, 128:256] = high
 
 
 def reach(cell, held):
@@ -302,7 +323,7 @@
 def edges_kernel(
     in_ref, displacement_ref, inverse_ref, slope_ref,
     psi_out, weight_ref, first_ref, second_ref,
-    psi_ref, carry_ref, psi_sem,
+    psi_ref, sum_ref, psi_sem,
 ):
     inverse = (inverse_ref[0], inverse_ref[1])
     slope = (slope_ref[0], slope_ref[1])
@@ -319,9 +340,9 @@
     held = {row: (weight_ref, slot) for slot, row in enumerate(EDGE_ROWS)}
 
     def cells(before_ref, after_ref):
-        for index in range(2):
-            collect(carry_ref, reach(index - 2, held), before_ref, index)
-            collect(carry_ref, reach(ROWS + index, held), after_ref, index)
+        jobs = [(reach(index - 2, held), before_ref, index) for index in range(2)]
+        jobs += [(reach(ROWS + index, held), after_ref, index) for index in range(2)]
+        collect(sum_ref, jobs)
 
     odd = lax.axis_index("gy") % 2
 
@@ -350,13 +371,13 @@
         out_specs=[ANY, VMEM, VMEM, VMEM],
         out_shape=[
             jax.ShapeDtypeStruct((3, ROWS, DEPTH, N), f32),
-            jax.ShapeDtypeStruct((4, 15, 2, HELD, 128), f32),
+            jax.ShapeDtypeStruct((4, 15, 2, DEPTH + PAD, 128), f32),
             halo,
             halo,
         ],
         scratch_shapes=[
             pltpu.VMEM((4, 3, DEPTH, N), f32),
-            pltpu.VMEM((2, 5, 8, 128), f32),
+            pltpu.VMEM((2, 5, 5, HELD + PAD, 128), f32),
             pltpu.SemaphoreType.DMA((4,)),
         ],
         compiler_params=pltpu.CompilerParams(vmem_limit_bytes=16 << 20),
@@ -367,7 +388,7 @@
 def inner_kernel(
     in_ref, displacement_ref, inverse_ref, slope_ref, psi_in, edge_ref,
     psi_out, out_ref,
-    psi_ref, weight_ref, carry_ref, psi_sem,
+    psi_ref, weight_ref, sum_ref, psi_sem,
 ):
     inverse = (inverse_ref[0], inverse_ref[1])
     slope = (slope_ref[0], slope_ref[1])
@@ -383,8 +404,7 @@
             copies.append(copy)
     held = {row: (edge_ref, slot) for slot, row in enumerate(EDGE_ROWS)}
     held.update({row: (weight_ref, row - 2) for row in range(2, ROWS - 2)})
-    for row in range(ROWS):
-        collect(carry_ref, reach(row, held), out_ref, row)
+    collect(sum_ref, [(reach(row, held), out_ref, row) for row in range(ROWS)])
     for copy in copies:
         copy.wait()
 
@@ -400,8 +420,8 @@
         ],
         scratch_shapes=[
             pltpu.VMEM((4, 3, DEPTH, N), f32),
-            pltpu.VMEM((4, 15, 2, HELD, 128), f32),
-            pltpu.VMEM((2, 5, 8, 128), f32),
+            pltpu.VMEM((4, 15, 2, DEPTH + PAD, 128), f32),
+            pltpu.VMEM((2, 5, 5, HELD + PAD, 128), f32),
             pltpu.SemaphoreType.DMA((4,)),
         ],
         input_output_aliases={4: 0},

time: 85 us -> 81.9 us (0.964)
  Pallas kernels: 22.8 us -> 18.3 us
  waiting for transfers between devices: 2.41 us -> 3.8 us
    pallas_call x1, Pallas kernels: 10.1 us -> 7.29 us  [inner(): pl.pallas_call(inner_kernel, in_specs=[VMEM] * 4 + [ANY, VMEM], out_specs...]
    pallas_call x1, Pallas kernels: 5.01 us -> 3.41 us  [edges(): pl.pallas_call(edges_kernel, in_specs=[VMEM] * 4, out_specs=[ANY, VMEM, V...]
    ppermute x1, waiting for transfers between devices: 0.01 us -> 1.55 us  [local(): lax.ppermute(second, 'gy', [(i, (i + (1 if i % 2 else -1)) % size_y) for...]
  transfers between devices with their start and end apart: 4 -> 4, of which waited for: 1 -> 2; matrix products, arithmetic and copies ran while one was open for 0% -> 0% of each run, Pallas kernels for 12% -> 9%
where the time goes in v1:
time: 81.9 us; the launch traced here: 81.7 us
  blocking collectives  53.8 us (66%)
  Pallas kernels  18.3 us (22%)
  starting transfers between devices  5.02 us (6%)
  waiting for transfers between devices  3.8 us (5%)
    all_to_all x1, blocking collectives, local(): lax.all_to_all(returned, both, split_axis=0, concat_axis=0, tiled=True)  28.7 us
    all_to_all x1, blocking collectives, local(): lax.all_to_all(spectra, both, split_axis=0, concat_axis=0, tiled=True)  25.1 us
    pallas_call x1, Pallas kernels, inner(): pl.pallas_call(inner_kernel, in_specs=[VMEM] * 4 + [ANY, VMEM], out_specs...  7.29 us
    pallas_call x1, Pallas kernels, lines(): pl.pallas_call(lines_kernel, in_specs=[far] * 3, out_specs=pl.BlockSpec(m...  4.5 us
    pallas_call x1, Pallas kernels, edges(): pl.pallas_call(edges_kernel, in_specs=[VMEM] * 4, out_specs=[ANY, VMEM, V...  3.41 us
    pallas_call x1, Pallas kernels, planes(): pl.pallas_call(planes_kernel, in_specs=[whole] * 6, out_specs=whole, out_...  2.27 us
    ppermute x1, waiting for transfers between devices, local(): right = lax.ppermute(side, 'gz', down)  2.24 us
    ppermute x1, starting transfers between devices, local(): lax.ppermute(second, 'gy', [(i, (i + (1 if i % 2 else -1)) % size_y) for...  1.82 us
  transfers between devices with their start and end apart: 4, of which 2 were waited for; matrix products, arithmetic and copies ran while one was open for 0% of the time, Pallas kernels for 9%

profile of v1, /device:TPU:1, one launch (start us, length us, event | category | flops | bytes accessed | tf_op | source)
XLA Modules:
  0.0 81.7 jit_solution(18225568634849656566)
XLA Ops:
  0.6 0.0 copy-start.1
  0.6 0.0 copy-start.2
  0.7 0.0 copy-start.3
  0.7 0.0 copy-start.4
  0.7 0.0 copy-start.5
  0.7 4.5 %lines.1 = f32[1024,128]{1,0:T(8,128)} custom-call(bf16[6,8,64,256]{3,2,1,0:T(8,128)(2,1)} %one_in.1, bf16[6,8,64,256]{3,2,1,0:T(8,128)(2,1)} %two_in.1, bf16[2,256,256]{2,1,0:T(8,128)(2,1)} %constant.10.clone.table_in.forward_ref), custom_call_target="tpu_custom_call" | custom-call | tf_op jit(solution)/shard_map/lines/pallas_call | solution.py:131
  5.2 25.1 %all_to_all.10 = f32[128,8,128]{2,1,0:T(8,128)S(1)} all-to-all(f32[128,8,128]{2,1,0:T(8,128)} %bitcast.8), channel_id=1, replica_groups=mesh['gy'=32,'gz'=4] {'gy','gz'}, dimensions={0} | all-to-all | bytes 1048576 | tf_op jit(solution)/shard_map/all_to_all | solution.py:490
  30.3 0.0 copy-done.1
  30.3 0.0 copy-done.2
  30.3 0.0 copy-done.3
  30.3 0.0 copy-done.4
  30.3 0.0 copy-done.5
  30.3 2.3 %planes.1 = f32[32,4,24,128]{3,2,1,0:T(8,128)S(1)} custom-call(f32[32,4,8,128]{3,2,1,0:T(8,128)S(1)} %bitcast.7, bf16[2,256,256]{2,1,0:T(8,128)(2,1)S(1)} %copy-done.3, bf16[2,256,256]{2,1,0:T(8,128)(2,1)S(1)} %copy-done.2, bf16[2,256,256]{2,1,0:T(8,128)(2,1)S(1)} %copy-done.1, bf16[2,256,256]{2,1,0:T(8,128)(2,1)S(1)} %copy-done.5, ...), custom_call_target="tpu_custom_call" | custom-call | tf_op jit(solution)/shard_map/planes/pallas_call | solution.py:202
  32.6 0.0 copy-start
  32.6 28.7 %all_to_all.11 = f32[128,24,128]{2,1,0:T(8,128)S(1)} all-to-all(f32[128,24,128]{2,1,0:T(8,128)S(1)} %bitcast.6), channel_id=1, replica_groups=mesh['gy'=32,'gz'=4] {'gy','gz'}, dimensions={0} | all-to-all | bytes 3145728 | tf_op jit(solution)/shard_map/all_to_all | solution.py:493
  61.3 0.0 copy-done
  61.3 3.4 %edges.1 = (f32[3,8,64,256]{3,2,1,0:T(8,128)}, f32[4,15,2,72,128]{4,3,2,1,0:T(8,128)S(1)}, f32[2,72,256]{2,1,0:T(8,128)S(1)}, f32[2,72,256]{2,1,0:T(8,128)S(1)}) custom-call(f32[3072,128]{1,0:T(8,128)S(1)} %bitcast.4, f32[3,8,64,256]{3,2,1,0:T(8,128)S(1)} %copy-done, bf16[2,256,256]{2,1,0:T(8,128)(2,1)S(1)} %copy-done.2, bf16[2,256,256]{2,1,0:T(8,128)(2,1)S(1)} %copy-done.1), custom_call_target="tpu_custom_call" | custom-call | tf_op jit(solution)/shard_map/edges/pallas_call | solution.py:368
  64.7 1.4 %collective-permute-start = (f32[2,72,256]{2,1,0:T(8,128)S(1)}, f32[2,72,256]{2,1,0:T(8,128)S(1)}, u32[]{:S(2)}, u32[]{:S(2)}) collective-permute-start(f32[2,72,256]{2,1,0:T(8,128)S(1)} %get-tuple-element.12), channel_id=1, source_target_pairs={{0,4},{4,0},{8,12},{12,8},{16,20},{20,16},{24,28},{28,24},{32,36},... | collective-permute-start | bytes 442376 | tf_op jit(solution)/shard_map/ppermute | solution.py:497
  66.1 1.8 %collective-permute-start.1 = (f32[2,72,256]{2,1,0:T(8,128)S(1)}, f32[2,72,256]{2,1,0:T(8,128)S(1)}, u32[]{:S(2)}, u32[]{:S(2)}) collective-permute-start(f32[2,72,256]{2,1,0:T(8,128)S(1)} %get-tuple-element.13), channel_id=1, source_target_pairs={{0,124},{4,8},{8,4},{12,16},{16,12},{20,24},{24,20},{28,32},{32,28... | collective-permute-start | bytes 442376 | tf_op jit(solution)/shard_map/ppermute | solution.py:498
  67.9 7.3 %inner.1 = (f32[3,8,64,256]{3,2,1,0:T(8,128)}, f32[8,72,256]{2,1,0:T(8,128)S(1)}) custom-call(f32[3072,128]{1,0:T(8,128)S(1)} %bitcast.5, f32[3,8,64,256]{3,2,1,0:T(8,128)S(1)} %copy-done, bf16[2,256,256]{2,1,0:T(8,128)(2,1)S(1)} %copy-done.2, bf16[2,256,256]{2,1,0:T(8,128)(2,1)S(1)} %copy-done.1, ...), custom_call_target="tpu_custom_call", output_to_operand_aliasing={{0}: (4, {})} | custom-call | tf_op jit(solution)/shard_map/inner/pallas_call | solution.py:413
  75.2 0.0 collective-permute-done.first_ref
  75.2 1.6 %collective-permute-done.1.second_ref = f32[2,72,256]{2,1,0:T(8,128)S(1)} collective-permute-done((f32[2,72,256]{2,1,0:T(8,128)S(1)}, f32[2,72,256]{2,1,0:T(8,128)S(1)}, u32[]{:S(2)}, u32[]{:S(2)}) %collective-permute-start.1) | collective-permute-done | bytes 147488 | tf_op jit(solution)/shard_map/ppermute | solution.py:498
  76.8 1.4 %collective-permute-start.3 = (f32[8,8,256]{2,1,0:T(8,128)S(1)}, f32[8,8,256]{2,1,0:T(8,128)S(1)}, u32[]{:S(2)}, u32[]{:S(2)}) collective-permute-start(f32[8,8,256]{2,1,0:T(8,128)S(1)} %sides.1), channel_id=1, source_target_pairs={{1,0},{2,1},{3,2},{0,3},{5,4},{6,5},{7,6},{4,7},{9,8},{10,9},{11,1... | collective-permute-start | bytes 196616 | tf_op jit(solution)/shard_map/ppermute | solution.py:506
  78.2 0.4 collective-permute-start.2
  78.6 2.2 %collective-permute-done.3.right_ref = f32[8,8,256]{2,1,0:T(8,128)S(1)} collective-permute-done((f32[8,8,256]{2,1,0:T(8,128)S(1)}, f32[8,8,256]{2,1,0:T(8,128)S(1)}, u32[]{:S(2)}, u32[]{:S(2)}) %collective-permute-start.3) | collective-permute-done | bytes 65568 | tf_op jit(solution)/shard_map/ppermute | solution.py:506
  80.9 0.0 collective-permute-done.2.left_ref
  80.9 0.9 %total.1 = f32[8,64,256]{2,1,0:T(8,128)} custom-call(f32[8,72,256]{2,1,0:T(8,128)S(1)} %get-tuple-element.11.cell_ref, f32[2,72,256]{2,1,0:T(8,128)S(1)} %collective-permute-done.first_ref, f32[2,72,256]{2,1,0:T(8,128)S(1)} %collective-permute-done.1.second_ref, f32[8,8,256]{2,1,0:T(8,128)S(1)} %collective-permute-done.2.left_ref, ...), custom_call_target="tpu_custom_call" | custom-call | tf_op jit(solution)/shard_map/total/pallas_call | solution.py:476
  (1 shorter events, 0.0 us)
Async XLA Ops:
  0.6 29.6 %copy-start.1 = (bf16[2,256,256]{2,1,0:T(8,128)(2,1)S(1)}, bf16[2,256,256]{2,1,0:T(8,128)(2,1)}, u32[]{:S(2)}) copy-start(bf16[2,256,256]{2,1,0:T(8,128)(2,1)} %constant.12.clone.slope_ref) | copy-start | bytes 786436
  0.6 29.6 %copy-start.2 = (bf16[2,256,256]{2,1,0:T(8,128)(2,1)S(1)}, bf16[2,256,256]{2,1,0:T(8,128)(2,1)}, u32[]{:S(2)}) copy-start(bf16[2,256,256]{2,1,0:T(8,128)(2,1)} %constant.11.clone.inverse_ref) | copy-start | bytes 786436
  0.7 29.6 %copy-start.3 = (bf16[2,256,256]{2,1,0:T(8,128)(2,1)S(1)}, bf16[2,256,256]{2,1,0:T(8,128)(2,1)}, u32[]{:S(2)}) copy-start(bf16[2,256,256]{2,1,0:T(8,128)(2,1)} %constant.10.clone.table_in.forward_ref) | copy-start | bytes 786436
  0.7 29.6 %copy-start.4 = (bf16[2,256,256]{2,1,0:T(8,128)(2,1)S(1)}, bf16[2,256,256]{2,1,0:T(8,128)(2,1)}, u32[]{:S(2)}) copy-start(bf16[2,256,256]{2,1,0:T(8,128)(2,1)} %constant.14.clone.slope_t_ref) | copy-start | bytes 786436
  0.7 29.6 %copy-start.5 = (bf16[2,256,256]{2,1,0:T(8,128)(2,1)S(1)}, bf16[2,256,256]{2,1,0:T(8,128)(2,1)}, u32[]{:S(2)}) copy-start(bf16[2,256,256]{2,1,0:T(8,128)(2,1)} %constant.13.clone.inverse_t_ref) | copy-start | bytes 786436
  32.6 28.7 %copy-start = (f32[3,8,64,256]{3,2,1,0:T(8,128)S(1)}, f32[3,8,64,256]{3,2,1,0:T(8,128)}, u32[]{:S(2)}) copy-start(f32[3,8,64,256]{3,2,1,0:T(8,128)} %displacement_ref.3) | copy-start | bytes 4718596
  64.7 10.5 %collective-permute-start = (f32[2,72,256]{2,1,0:T(8,128)S(1)}, f32[2,72,256]{2,1,0:T(8,128)S(1)}, u32[]{:S(2)}, u32[]{:S(2)}) collective-permute-start(f32[2,72,256]{2,1,0:T(8,128)S(1)} %get-tuple-element.12), channel_id=1, source_target_pairs={{0,4},{4,0},{8,12},{12,8},{16,20},{20,16},{24,28},{28,24},{32,36},... | collective-permute-start | bytes 442376 | tf_op jit(solution)/shard_map/ppermute | solution.py:497
  66.1 10.7 %collective-permute-start.1 = (f32[2,72,256]{2,1,0:T(8,128)S(1)}, f32[2,72,256]{2,1,0:T(8,128)S(1)}, u32[]{:S(2)}, u32[]{:S(2)}) collective-permute-start(f32[2,72,256]{2,1,0:T(8,128)S(1)} %get-tuple-element.13), channel_id=1, source_target_pairs={{0,124},{4,8},{8,4},{12,16},{16,12},{20,24},{24,20},{28,32},{32,28... | collective-permute-start | bytes 442376 | tf_op jit(solution)/shard_map/ppermute | solution.py:498
  76.8 4.1 %collective-permute-start.3 = (f32[8,8,256]{2,1,0:T(8,128)S(1)}, f32[8,8,256]{2,1,0:T(8,128)S(1)}, u32[]{:S(2)}, u32[]{:S(2)}) collective-permute-start(f32[8,8,256]{2,1,0:T(8,128)S(1)} %sides.1), channel_id=1, source_target_pairs={{1,0},{2,1},{3,2},{0,3},{5,4},{6,5},{7,6},{4,7},{9,8},{10,9},{11,1... | collective-permute-start | bytes 196616 | tf_op jit(solution)/shard_map/ppermute | solution.py:506
  78.2 2.7 %collective-permute-start.2 = (f32[8,8,256]{2,1,0:T(8,128)S(1)}, f32[8,8,256]{2,1,0:T(8,128)S(1)}, u32[]{:S(2)}, u32[]{:S(2)}) collective-permute-start(f32[8,8,256]{2,1,0:T(8,128)S(1)} %sides.1), channel_id=1, source_target_pairs={{0,1},{1,2},{2,3},{3,0},{4,5},{5,6},{6,7},{7,4},{8,9},{9,10},{10,1... | collective-permute-start | bytes 196616 | tf_op jit(solution)/shard_map/ppermute | solution.py:505

commit v2 on v1

--- a/solution.py
+++ b/solution.py
@@ -139,9 +139,13 @@
             pltpu.VMEM((2, N, N), bf16),
             pltpu.SemaphoreType.DMA((ROWS + 1,)),
         ],
-        compiler_params=pltpu.CompilerParams(vmem_limit_bytes=61 << 20),
+        compiler_params=pltpu.CompilerParams(vmem_limit_bytes=16 << 20),
         name="lines",
-    )(one, two, jnp.asarray(split_table(forward_table)))
+    )(
+        pltpu.with_memory_space_constraint(one, pltpu.HBM),
+        pltpu.with_memory_space_constraint(two, pltpu.HBM),
+        pltpu.with_memory_space_constraint(jnp.asarray(split_table(forward_table)), pltpu.HBM),
+    )
 
 
 def planes_kernel(in_ref, forward_ref, inverse_ref, slope_ref, inverse_t_ref, slope_t_ref, out_ref):
@@ -193,12 +197,8 @@
             out_ref[:, g + 1, field * ROWS : (field + 1) * ROWS, :] = odd.reshape(32, ROWS, 128)
 
 
-def planes(values):
+def planes(values, tables):
     whole = pl.BlockSpec(memory_space=pltpu.VMEM)
-    tables = [
-        jnp.asarray(split_table(t))
-        for t in (forward_table, inverse_table, slope_table, inverse_table.T, slope_table.T)
-    ]
     return pl.pallas_call(
         planes_kernel,
         in_specs=[whole] * 6,
@@ -216,13 +216,21 @@
 
 
 def tile_weights(moved):
+    cell = jnp.floor(moved)
+    rise = moved - cell
+    fall = 1.0 - rise
+    rise2, fall2 = rise * rise, fall * fall
+    outer_low, outer_high = rise2 * rise, fall2 * fall
+    inner_high = 4.0 - 3.0 * (rise2 * (1.0 + fall))
+    inner_low = 4.0 - 3.0 * (fall2 * (1.0 + rise))
+    pieces = (outer_low, inner_low, inner_high, outer_high)
+    at = {n: cell == n for n in range(-4, 4)}
     weights = []
-    for shift in range(5):
-        offset = moved + (shift - 2.0) if shift != 2 else moved
-        outer = jnp.maximum(2.0 - jnp.abs(offset), 0.0)
-        weights.append(
-            jnp.minimum(4.0 - 3.0 * ((offset * offset) * outer), (outer * outer) * outer)
-        )
+    for offset in range(-2, 3):
+        weight = jnp.zeros_like(moved)
+        for piece, value in zip(range(-2, 2), pieces):
+            weight = jnp.where(at[piece - offset], value, weight)
+        weights.append(weight)
     return weights
 
 
@@ -322,7 +330,7 @@
 
 def edges_kernel(
     in_ref, displacement_ref, inverse_ref, slope_ref,
-    psi_out, weight_ref, first_ref, second_ref,
+    psi_out, weight_ref, second_ref, first_ref,
     psi_ref, sum_ref, psi_sem,
 ):
     inverse = (inverse_ref[0], inverse_ref[1])
@@ -430,46 +438,52 @@
     )(values, displacement, *tables, psi, weights)
 
 
-def halos(first_ref, second_ref, where):
-    even = lax.axis_index("gy") % 2 == 0
-    first, second = first_ref[:, where, :], second_ref[:, where, :]
+def ordered(axis, first, second):
+    even = lax.axis_index(axis) % 2 == 0
     return jnp.where(even, second, first), jnp.where(even, first, second)
 
 
-def sides_kernel(cell_ref, first_ref, second_ref, out_ref):
-    low, high = halos(first_ref, second_ref, slice(None))
+def sides_kernel(cell_ref, first_ref, second_ref, low_ref, high_ref):
+    low, high = ordered("gy", first_ref[...], second_ref[...])
     side = cell_ref[...]
-    out_ref[0:2] = side[0:2] + low
-    out_ref[2 : ROWS - 2] = side[2 : ROWS - 2]
-    out_ref[ROWS - 2 :] = side[ROWS - 2 :] + high
+    side = jnp.concatenate(
+        [side[0:2] + low, side[2 : ROWS - 2], side[ROWS - 2 :] + high], axis=0
+    )
+    above, below = side[:, 0:2, :], side[:, PAD - 2 :, :]
+    even = lax.axis_index("gz") % 2 == 0
+    low_ref[...] = jnp.where(even, above, below)
+    high_ref[...] = jnp.where(even, below, above)
 
 
 def sides(cells, first, second):
     last = DEPTH // PAD
     block = lambda rows: pl.BlockSpec((rows, PAD, N), lambda i: (0, last, 0))
+    side = jax.ShapeDtypeStruct((ROWS, 2, N), f32)
     return pl.pallas_call(
         sides_kernel,
         grid=(1,),
         in_specs=[block(ROWS), block(2), block(2)],
-        out_specs=pl.BlockSpec((ROWS, PAD, N), lambda i: (0, 0, 0)),
-        out_shape=jax.ShapeDtypeStruct((ROWS, PAD, N), f32),
+        out_specs=[pl.BlockSpec((ROWS, 2, N), lambda i: (0, 0, 0))] * 2,
+        out_shape=[side, side],
         compiler_params=pltpu.CompilerParams(vmem_limit_bytes=8 << 20),
         name="sides",
     )(cells, first, second)
 
 
-def sum_kernel(cell_ref, first_ref, second_ref, left_ref, right_ref, out_ref):
-    low, high = halos(first_ref, second_ref, slice(0, DEPTH))
-    sub = lax.broadcasted_iota(jnp.int32, (PAD, N), 0)
+def sum_kernel(cell_ref, first_ref, second_ref, near_ref, far_ref, out_ref):
+    low, high = ordered("gy", first_ref[:, :DEPTH, :], second_ref[:, :DEPTH, :])
+    left, right = ordered("gz", near_ref[...], far_ref[...])
     for row in range(ROWS):
         value = cell_ref[row, :DEPTH, :] - 1.0
         if row < 2:
             value = value + low[row]
         if row >= ROWS - 2:
             value = value + high[row - ROWS + 2]
-        out_ref[row, 0:8, :] = value[0:8] + jnp.where(sub < 2, left_ref[row], 0.0)
+        out_ref[row, 0:2, :] = value[0:2] + left[row]
+        out_ref[row, 2:8, :] = value[2:8]
         out_ref[row, 8:56, :] = value[8:56]
-        out_ref[row, 56:64, :] = value[56:64] + jnp.where(sub >= 6, right_ref[row], 0.0)
+        out_ref[row, 56:62, :] = value[56:62]
+        out_ref[row, 62:64, :] = value[62:64] + right[row]
 
 
 def total(*parts):
@@ -483,28 +497,35 @@
     )(*parts)
 
 
+def swap(value, axis, rounds):
+    size = lax.axis_size(axis)
+    return lax.ppermute(
+        value, axis, [(i, (i + (1 if i % 2 == rounds else -1)) % size) for i in range(size)]
+    )
+
+
 def local(hessian_one, hessian_two, displacement):
-    size_y, size_z = lax.axis_size("gy"), lax.axis_size("gz")
     both = ("gy", "gz")
-    spectra = lines(hessian_one, hessian_two).reshape(HALF, ROWS, 128)
+    tables = [
+        jnp.asarray(split_table(t))
+        for t in (forward_table, inverse_table, slope_table, inverse_table.T, slope_table.T)
+    ]
+    spectra = lines(hessian_one, hessian_two)
+    spectra = spectra.reshape(HALF, ROWS, 128)
     spectra = lax.all_to_all(spectra, both, split_axis=0, concat_axis=0, tiled=True)
-    returned = planes(spectra.reshape(32, 4, ROWS, 128))
+    returned = planes(spectra.reshape(32, 4, ROWS, 128), tables)
     returned = returned.reshape(HALF, 3 * ROWS, 128)
     returned = lax.all_to_all(returned, both, split_axis=0, concat_axis=0, tiled=True)
     returned = returned.reshape(HALF * 3 * ROWS, 128)
-    tables = [jnp.asarray(split_table(t)) for t in (inverse_table, slope_table)]
-    psi, weights, first, second = edges(returned, displacement, tables)
-    first = lax.ppermute(first, "gy", [(i, i ^ 1) for i in range(size_y)])
-    second = lax.ppermute(
-        second, "gy", [(i, (i + (1 if i % 2 else -1)) % size_y) for i in range(size_y)]
-    )
+    tables = tables[1:3]
+    psi, weights, second, first = edges(returned, displacement, tables)
+    second = swap(second, "gy", 1)
+    first = swap(first, "gy", 0)
     psi, cells = inner(returned, displacement, tables, psi, weights)
-    side = sides(cells, first, second)
-    up = [(i, (i + 1) % size_z) for i in range(size_z)]
-    down = [(j, i) for i, j in up]
-    left = lax.ppermute(side, "gz", up)
-    right = lax.ppermute(side, "gz", down)
-    density = total(cells, first, second, left, right)
+    near, far = sides(cells, first, second)
+    far = swap(far, "gz", 1)
+    near = swap(near, "gz", 0)
+    density = total(cells, first, second, near, far)
     return psi, density
 
 

time: 81.9 us -> 81.1 us (level)
  Pallas kernels: 18.3 us -> 17.1 us
  waiting for transfers between devices: 3.8 us -> 4.97 us
    ppermute x4, waiting for transfers between devices: 3.8 us -> 4.97 us  [swap(): lax.ppermute(value, axis, [(i, (i + (1 if i % 2 == rounds else -1)) % siz...]
  transfers between devices with their start and end apart: 4 -> 4, of which waited for: 2 -> 3; matrix products, arithmetic and copies ran while one was open for 0% -> 0% of each run, Pallas kernels for 9% -> 9%
where the time goes in v2:
time: 81.1 us; the launch traced here: 81 us
  blocking collectives  53.6 us (66%)
  Pallas kernels  17.1 us (21%)
  waiting for transfers between devices  4.97 us (6%)
  starting transfers between devices  4.59 us (6%)
    all_to_all x1, blocking collectives, local(): lax.all_to_all(returned, both, split_axis=0, concat_axis=0, tiled=True)  28.7 us
    all_to_all x1, blocking collectives, local(): lax.all_to_all(spectra, both, split_axis=0, concat_axis=0, tiled=True)  24.8 us
    pallas_call x1, Pallas kernels, inner(): pl.pallas_call(inner_kernel, in_specs=[VMEM] * 4 + [ANY, VMEM], out_specs...  7.04 us
    ppermute x4, waiting for transfers between devices, swap(): lax.ppermute(value, axis, [(i, (i + (1 if i % 2 == rounds else -1)) % siz...  4.97 us
    ppermute x4, starting transfers between devices, swap(): lax.ppermute(value, axis, [(i, (i + (1 if i % 2 == rounds else -1)) % siz...  4.59 us
    pallas_call x1, Pallas kernels, lines(): pl.pallas_call(lines_kernel, in_specs=[far] * 3, out_specs=pl.BlockSpec(m...  3.71 us
    pallas_call x1, Pallas kernels, edges(): pl.pallas_call(edges_kernel, in_specs=[VMEM] * 4, out_specs=[ANY, VMEM, V...  3.16 us
    pallas_call x1, Pallas kernels, planes(): pl.pallas_call(planes_kernel, in_specs=[whole] * 6, out_specs=whole, out_...  2.27 us
  transfers between devices with their start and end apart: 4, of which 3 were waited for; matrix products, arithmetic and copies ran while one was open for 0% of the time, Pallas kernels for 9%

profile of v2, /device:TPU:1, one launch (start us, length us, event | category | flops | bytes accessed | tf_op | source)
XLA Modules:
  0.0 81.0 jit_solution(10929303943584852045)
XLA Ops:
  0.6 0.0 copy-start.1
  0.6 0.0 copy-start.2
  0.7 0.0 copy-start.3
  0.7 0.0 copy-start.4
  0.7 0.0 copy-start.5
  0.7 3.7 %lines.1 = f32[1024,128]{1,0:T(8,128)S(1)} custom-call(bf16[6,8,64,256]{3,2,1,0:T(8,128)(2,1)} %one_in.1, bf16[6,8,64,256]{3,2,1,0:T(8,128)(2,1)} %two_in.1, bf16[2,256,256]{2,1,0:T(8,128)(2,1)} %constant.10.clone.table_in.forward_ref), custom_call_target="tpu_custom_call" | custom-call | tf_op jit(solution)/shard_map/lines/pallas_call | solution.py:131
  4.4 24.8 %all_to_all.10 = f32[128,8,128]{2,1,0:T(8,128)S(1)} all-to-all(f32[128,8,128]{2,1,0:T(8,128)S(1)} %bitcast.7), channel_id=1, replica_groups=mesh['gy'=32,'gz'=4] {'gy','gz'}, dimensions={0} | all-to-all | bytes 1048576 | tf_op jit(solution)/shard_map/all_to_all | solution.py:515
  29.3 0.0 copy-done.1
  29.3 0.0 copy-done.2
  29.3 0.0 copy-done.3
  29.3 0.0 copy-done.4
  29.3 0.0 copy-done.5
  29.3 2.3 %planes.1 = f32[32,4,24,128]{3,2,1,0:T(8,128)S(1)} custom-call(f32[32,4,8,128]{3,2,1,0:T(8,128)S(1)} %bitcast.8, bf16[2,256,256]{2,1,0:T(8,128)(2,1)S(1)} %copy-done.3, bf16[2,256,256]{2,1,0:T(8,128)(2,1)S(1)} %copy-done.2, bf16[2,256,256]{2,1,0:T(8,128)(2,1)S(1)} %copy-done.1, bf16[2,256,256]{2,1,0:T(8,128)(2,1)S(1)} %copy-done.5, ...), custom_call_target="tpu_custom_call" | custom-call | tf_op jit(solution)/shard_map/planes/pallas_call | solution.py:202
  31.6 0.0 copy-start
  31.6 28.7 %all_to_all.11 = f32[128,24,128]{2,1,0:T(8,128)S(1)} all-to-all(f32[128,24,128]{2,1,0:T(8,128)S(1)} %bitcast.6), channel_id=1, replica_groups=mesh['gy'=32,'gz'=4] {'gy','gz'}, dimensions={0} | all-to-all | bytes 3145728 | tf_op jit(solution)/shard_map/all_to_all | solution.py:518
  60.3 0.0 copy-done
  60.3 3.2 %edges.1 = (f32[3,8,64,256]{3,2,1,0:T(8,128)}, f32[4,15,2,72,128]{4,3,2,1,0:T(8,128)S(1)}, f32[2,72,256]{2,1,0:T(8,128)S(1)}, f32[2,72,256]{2,1,0:T(8,128)S(1)}) custom-call(f32[3072,128]{1,0:T(8,128)S(1)} %bitcast.4, f32[3,8,64,256]{3,2,1,0:T(8,128)S(1)} %copy-done, bf16[2,256,256]{2,1,0:T(8,128)(2,1)S(1)} %copy-done.2, bf16[2,256,256]{2,1,0:T(8,128)(2,1)S(1)} %copy-done.1), custom_call_target="tpu_custom_call" | custom-call | tf_op jit(solution)/shard_map/edges/pallas_call | solution.py:376
  63.5 1.4 %collective-permute-start = (f32[2,72,256]{2,1,0:T(8,128)S(1)}, f32[2,72,256]{2,1,0:T(8,128)S(1)}, u32[]{:S(2)}, u32[]{:S(2)}) collective-permute-start(f32[2,72,256]{2,1,0:T(8,128)S(1)} %get-tuple-element.14), channel_id=1, source_target_pairs={{0,4},{4,0},{8,12},{12,8},{16,20},{20,16},{24,28},{28,24},{32,36},... | collective-permute-start | bytes 442376 | tf_op jit(solution)/shard_map/ppermute | solution.py:502
  64.9 1.8 %collective-permute-start.1 = (f32[2,72,256]{2,1,0:T(8,128)S(1)}, f32[2,72,256]{2,1,0:T(8,128)S(1)}, u32[]{:S(2)}, u32[]{:S(2)}) collective-permute-start(f32[2,72,256]{2,1,0:T(8,128)S(1)} %get-tuple-element.15), channel_id=1, source_target_pairs={{0,124},{4,8},{8,4},{12,16},{16,12},{20,24},{24,20},{28,32},{32,28... | collective-permute-start | bytes 442376 | tf_op jit(solution)/shard_map/ppermute | solution.py:502
  66.7 7.0 %inner.1 = (f32[3,8,64,256]{3,2,1,0:T(8,128)}, f32[8,72,256]{2,1,0:T(8,128)S(1)}) custom-call(f32[3072,128]{1,0:T(8,128)S(1)} %bitcast.5, f32[3,8,64,256]{3,2,1,0:T(8,128)S(1)} %copy-done, bf16[2,256,256]{2,1,0:T(8,128)(2,1)S(1)} %copy-done.2, bf16[2,256,256]{2,1,0:T(8,128)(2,1)S(1)} %copy-done.1, ...), custom_call_target="tpu_custom_call", output_to_operand_aliasing={{0}: (4, {})} | custom-call | tf_op jit(solution)/shard_map/inner/pallas_call | solution.py:421
  73.7 0.0 collective-permute-done.first_ref
  73.7 1.8 %collective-permute-done.1.second_ref = f32[2,72,256]{2,1,0:T(8,128)S(1)} collective-permute-done((f32[2,72,256]{2,1,0:T(8,128)S(1)}, f32[2,72,256]{2,1,0:T(8,128)S(1)}, u32[]{:S(2)}, u32[]{:S(2)}) %collective-permute-start.1) | collective-permute-done | bytes 147488 | tf_op jit(solution)/shard_map/ppermute | solution.py:502
  75.6 1.4 %collective-permute-start.2 = (f32[8,2,256]{2,1,0:T(2,128)S(1)}, f32[8,2,256]{2,1,0:T(2,128)S(1)}, u32[]{:S(2)}, u32[]{:S(2)}) collective-permute-start(f32[8,2,256]{2,1,0:T(2,128)S(1)} %get-tuple-element.16), channel_id=1, source_target_pairs={{0,1},{1,0},{2,3},{3,2},{4,5},{5,4},{6,7},{7,6},{8,9},{9,8},{10,11... | collective-permute-start | bytes 49160 | tf_op jit(solution)/shard_map/ppermute | solution.py:502
  77.0 0.0 collective-permute-start.3
  77.0 0.8 %collective-permute-done.2.near_ref = f32[8,2,256]{2,1,0:T(2,128)S(1)} collective-permute-done((f32[8,2,256]{2,1,0:T(2,128)S(1)}, f32[8,2,256]{2,1,0:T(2,128)S(1)}, u32[]{:S(2)}, u32[]{:S(2)}) %collective-permute-start.2) | collective-permute-done | bytes 16416 | tf_op jit(solution)/shard_map/ppermute | solution.py:502
  77.8 2.3 %collective-permute-done.3.far_ref = f32[8,2,256]{2,1,0:T(2,128)S(1)} collective-permute-done((f32[8,2,256]{2,1,0:T(2,128)S(1)}, f32[8,2,256]{2,1,0:T(2,128)S(1)}, u32[]{:S(2)}, u32[]{:S(2)}) %collective-permute-start.3) | collective-permute-done | bytes 16416 | tf_op jit(solution)/shard_map/ppermute | solution.py:502
  80.1 0.9 %total.1 = f32[8,64,256]{2,1,0:T(8,128)} custom-call(f32[8,72,256]{2,1,0:T(8,128)S(1)} %get-tuple-element.13.cell_ref, f32[2,72,256]{2,1,0:T(8,128)S(1)} %collective-permute-done.first_ref, f32[2,72,256]{2,1,0:T(8,128)S(1)} %collective-permute-done.1.second_ref, f32[8,2,256]{2,1,0:T(2,128)S(1)} %collective-permute-done.2.near_ref, ...), custom_call_target="tpu_custom_call" | custom-call | tf_op jit(solution)/shard_map/total/pallas_call | solution.py:490
  (1 shorter events, 0.0 us)
Async XLA Ops:
  0.6 28.6 %copy-start.1 = (bf16[2,256,256]{2,1,0:T(8,128)(2,1)S(1)}, bf16[2,256,256]{2,1,0:T(8,128)(2,1)}, u32[]{:S(2)}) copy-start(bf16[2,256,256]{2,1,0:T(8,128)(2,1)} %constant.12.clone.slope_ref) | copy-start | bytes 786436
  0.6 28.6 %copy-start.2 = (bf16[2,256,256]{2,1,0:T(8,128)(2,1)S(1)}, bf16[2,256,256]{2,1,0:T(8,128)(2,1)}, u32[]{:S(2)}) copy-start(bf16[2,256,256]{2,1,0:T(8,128)(2,1)} %constant.11.clone.inverse_ref) | copy-start | bytes 786436
  0.7 28.6 %copy-start.3 = (bf16[2,256,256]{2,1,0:T(8,128)(2,1)S(1)}, bf16[2,256,256]{2,1,0:T(8,128)(2,1)}, u32[]{:S(2)}) copy-start(bf16[2,256,256]{2,1,0:T(8,128)(2,1)} %constant.10.clone.table_in.forward_ref) | copy-start | bytes 786436
  0.7 28.6 %copy-start.4 = (bf16[2,256,256]{2,1,0:T(8,128)(2,1)S(1)}, bf16[2,256,256]{2,1,0:T(8,128)(2,1)}, u32[]{:S(2)}) copy-start(bf16[2,256,256]{2,1,0:T(8,128)(2,1)} %constant.14.clone.slope_t_ref) | copy-start | bytes 786436
  0.7 28.6 %copy-start.5 = (bf16[2,256,256]{2,1,0:T(8,128)(2,1)S(1)}, bf16[2,256,256]{2,1,0:T(8,128)(2,1)}, u32[]{:S(2)}) copy-start(bf16[2,256,256]{2,1,0:T(8,128)(2,1)} %constant.13.clone.inverse_t_ref) | copy-start | bytes 786436
  31.6 28.7 %copy-start = (f32[3,8,64,256]{3,2,1,0:T(8,128)S(1)}, f32[3,8,64,256]{3,2,1,0:T(8,128)}, u32[]{:S(2)}) copy-start(f32[3,8,64,256]{3,2,1,0:T(8,128)} %displacement_ref.3) | copy-start | bytes 4718596
  63.5 10.3 %collective-permute-start = (f32[2,72,256]{2,1,0:T(8,128)S(1)}, f32[2,72,256]{2,1,0:T(8,128)S(1)}, u32[]{:S(2)}, u32[]{:S(2)}) collective-permute-start(f32[2,72,256]{2,1,0:T(8,128)S(1)} %get-tuple-element.14), channel_id=1, source_target_pairs={{0,4},{4,0},{8,12},{12,8},{16,20},{20,16},{24,28},{28,24},{32,36},... | collective-permute-start | bytes 442376 | tf_op jit(solution)/shard_map/ppermute | solution.py:502
  64.9 10.7 %collective-permute-start.1 = (f32[2,72,256]{2,1,0:T(8,128)S(1)}, f32[2,72,256]{2,1,0:T(8,128)S(1)}, u32[]{:S(2)}, u32[]{:S(2)}) collective-permute-start(f32[2,72,256]{2,1,0:T(8,128)S(1)} %get-tuple-element.15), channel_id=1, source_target_pairs={{0,124},{4,8},{8,4},{12,16},{16,12},{20,24},{24,20},{28,32},{32,28... | collective-permute-start | bytes 442376 | tf_op jit(solution)/shard_map/ppermute | solution.py:502
  75.6 2.2 %collective-permute-start.2 = (f32[8,2,256]{2,1,0:T(2,128)S(1)}, f32[8,2,256]{2,1,0:T(2,128)S(1)}, u32[]{:S(2)}, u32[]{:S(2)}) collective-permute-start(f32[8,2,256]{2,1,0:T(2,128)S(1)} %get-tuple-element.16), channel_id=1, source_target_pairs={{0,1},{1,0},{2,3},{3,2},{4,5},{5,4},{6,7},{7,6},{8,9},{9,8},{10,11... | collective-permute-start | bytes 49160 | tf_op jit(solution)/shard_map/ppermute | solution.py:502
  77.0 3.2 %collective-permute-start.3 = (f32[8,2,256]{2,1,0:T(2,128)S(1)}, f32[8,2,256]{2,1,0:T(2,128)S(1)}, u32[]{:S(2)}, u32[]{:S(2)}) collective-permute-start(f32[8,2,256]{2,1,0:T(2,128)S(1)} %get-tuple-element.17), channel_id=1, source_target_pairs={{0,3},{1,2},{2,1},{3,0},{4,7},{5,6},{6,5},{7,4},{8,11},{9,10},{10,... | collective-permute-start | bytes 49160 | tf_op jit(solution)/shard_map/ppermute | solution.py:502

commit v3 on v2

--- a/solution.py
+++ b/solution.py
@@ -7,6 +7,7 @@
 from jax.experimental import pallas as pl
 from jax.experimental.pallas import tpu as pltpu
 from jax.sharding import PartitionSpec as P
+
 
 N = 256
 HALF = N // 2
@@ -212,7 +213,6 @@
 PAD = 8
 HELD = DEPTH + 2 * PAD
 EDGE_ROWS = (0, 1, ROWS - 2, ROWS - 1)
-EVERY_ROW = tuple(range(ROWS))
 
 
 def tile_weights(moved):
@@ -532,4 +532,6 @@
 def solution(mesh):
     in_specs = (P(None, "gy", "gz", None), P(None, "gy", "gz", None), P(None, "gy", "gz", None))
     out_specs = (P(None, "gy", "gz", None), P("gy", "gz", None))
-    return jax.shard_map(local, mesh=mesh, in_specs=in_specs, out_specs=out_specs, check_vma=False)
+    return jax.shard_map(
+        local, mesh=mesh, in_specs=in_specs, out_specs=out_specs, check_vma=False
+    )

time: 81.1 us -> 81.1 us (level)
  no operation moved by 1% of the time
where the time goes in v3:
time: 81.1 us; the launch traced here: 81 us
  blocking collectives  53.6 us (66%)
  Pallas kernels  17.1 us (21%)
  waiting for transfers between devices  4.97 us (6%)
  starting transfers between devices  4.59 us (6%)
    all_to_all x1, blocking collectives, local(): lax.all_to_all(returned, both, split_axis=0, concat_axis=0, tiled=True)  28.7 us
    all_to_all x1, blocking collectives, local(): lax.all_to_all(spectra, both, split_axis=0, concat_axis=0, tiled=True)  24.8 us
    pallas_call x1, Pallas kernels, inner(): pl.pallas_call(inner_kernel, in_specs=[VMEM] * 4 + [ANY, VMEM], out_specs...  7.04 us
    ppermute x4, waiting for transfers between devices, swap(): lax.ppermute(value, axis, [(i, (i + (1 if i % 2 == rounds else -1)) % siz...  4.97 us
    ppermute x4, starting transfers between devices, swap(): lax.ppermute(value, axis, [(i, (i + (1 if i % 2 == rounds else -1)) % siz...  4.59 us
    pallas_call x1, Pallas kernels, lines(): pl.pallas_call(lines_kernel, in_specs=[far] * 3, out_specs=pl.BlockSpec(m...  3.71 us
    pallas_call x1, Pallas kernels, edges(): pl.pallas_call(edges_kernel, in_specs=[VMEM] * 4, out_specs=[ANY, VMEM, V...  3.16 us
    pallas_call x1, Pallas kernels, planes(): pl.pallas_call(planes_kernel, in_specs=[whole] * 6, out_specs=whole, out_...  2.27 us
  transfers between devices with their start and end apart: 4, of which 3 were waited for; matrix products, arithmetic and copies ran while one was open for 0% of the time, Pallas kernels for 9%

profile of v3, /device:TPU:1, one launch (start us, length us, event | category | flops | bytes accessed | tf_op | source)
XLA Modules:
  0.0 81.0 jit_solution(10929303943584852045)
XLA Ops:
  0.6 0.0 copy-start.1
  0.6 0.0 copy-start.2
  0.7 0.0 copy-start.3
  0.7 0.0 copy-start.4
  0.7 0.0 copy-start.5
  0.7 3.7 %lines.1 = f32[1024,128]{1,0:T(8,128)S(1)} custom-call(bf16[6,8,64,256]{3,2,1,0:T(8,128)(2,1)} %one_in.1, bf16[6,8,64,256]{3,2,1,0:T(8,128)(2,1)} %two_in.1, bf16[2,256,256]{2,1,0:T(8,128)(2,1)} %constant.10.clone.table_in.forward_ref), custom_call_target="tpu_custom_call" | custom-call | tf_op jit(solution)/shard_map/lines/pallas_call | solution.py:132
  4.4 24.8 %all_to_all.10 = f32[128,8,128]{2,1,0:T(8,128)S(1)} all-to-all(f32[128,8,128]{2,1,0:T(8,128)S(1)} %bitcast.7), channel_id=1, replica_groups=mesh['gy'=32,'gz'=4] {'gy','gz'}, dimensions={0} | all-to-all | bytes 1048576 | tf_op jit(solution)/shard_map/all_to_all | solution.py:515
  29.3 0.0 copy-done.1
  29.3 0.0 copy-done.2
  29.3 0.0 copy-done.3
  29.3 0.0 copy-done.4
  29.3 0.0 copy-done.5
  29.3 2.3 %planes.1 = f32[32,4,24,128]{3,2,1,0:T(8,128)S(1)} custom-call(f32[32,4,8,128]{3,2,1,0:T(8,128)S(1)} %bitcast.8, bf16[2,256,256]{2,1,0:T(8,128)(2,1)S(1)} %copy-done.3, bf16[2,256,256]{2,1,0:T(8,128)(2,1)S(1)} %copy-done.2, bf16[2,256,256]{2,1,0:T(8,128)(2,1)S(1)} %copy-done.1, bf16[2,256,256]{2,1,0:T(8,128)(2,1)S(1)} %copy-done.5, ...), custom_call_target="tpu_custom_call" | custom-call | tf_op jit(solution)/shard_map/planes/pallas_call | solution.py:203
  31.6 0.0 copy-start
  31.6 28.7 %all_to_all.11 = f32[128,24,128]{2,1,0:T(8,128)S(1)} all-to-all(f32[128,24,128]{2,1,0:T(8,128)S(1)} %bitcast.6), channel_id=1, replica_groups=mesh['gy'=32,'gz'=4] {'gy','gz'}, dimensions={0} | all-to-all | bytes 3145728 | tf_op jit(solution)/shard_map/all_to_all | solution.py:518
  60.3 0.0 copy-done
  60.3 3.2 %edges.1 = (f32[3,8,64,256]{3,2,1,0:T(8,128)}, f32[4,15,2,72,128]{4,3,2,1,0:T(8,128)S(1)}, f32[2,72,256]{2,1,0:T(8,128)S(1)}, f32[2,72,256]{2,1,0:T(8,128)S(1)}) custom-call(f32[3072,128]{1,0:T(8,128)S(1)} %bitcast.4, f32[3,8,64,256]{3,2,1,0:T(8,128)S(1)} %copy-done, bf16[2,256,256]{2,1,0:T(8,128)(2,1)S(1)} %copy-done.2, bf16[2,256,256]{2,1,0:T(8,128)(2,1)S(1)} %copy-done.1), custom_call_target="tpu_custom_call" | custom-call | tf_op jit(solution)/shard_map/edges/pallas_call | solution.py:376
  63.5 1.4 %collective-permute-start = (f32[2,72,256]{2,1,0:T(8,128)S(1)}, f32[2,72,256]{2,1,0:T(8,128)S(1)}, u32[]{:S(2)}, u32[]{:S(2)}) collective-permute-start(f32[2,72,256]{2,1,0:T(8,128)S(1)} %get-tuple-element.14), channel_id=1, source_target_pairs={{0,4},{4,0},{8,12},{12,8},{16,20},{20,16},{24,28},{28,24},{32,36},... | collective-permute-start | bytes 442376 | tf_op jit(solution)/shard_map/ppermute | solution.py:502
  64.9 1.8 %collective-permute-start.1 = (f32[2,72,256]{2,1,0:T(8,128)S(1)}, f32[2,72,256]{2,1,0:T(8,128)S(1)}, u32[]{:S(2)}, u32[]{:S(2)}) collective-permute-start(f32[2,72,256]{2,1,0:T(8,128)S(1)} %get-tuple-element.15), channel_id=1, source_target_pairs={{0,124},{4,8},{8,4},{12,16},{16,12},{20,24},{24,20},{28,32},{32,28... | collective-permute-start | bytes 442376 | tf_op jit(solution)/shard_map/ppermute | solution.py:502
  66.7 7.0 %inner.1 = (f32[3,8,64,256]{3,2,1,0:T(8,128)}, f32[8,72,256]{2,1,0:T(8,128)S(1)}) custom-call(f32[3072,128]{1,0:T(8,128)S(1)} %bitcast.5, f32[3,8,64,256]{3,2,1,0:T(8,128)S(1)} %copy-done, bf16[2,256,256]{2,1,0:T(8,128)(2,1)S(1)} %copy-done.2, bf16[2,256,256]{2,1,0:T(8,128)(2,1)S(1)} %copy-done.1, ...), custom_call_target="tpu_custom_call", output_to_operand_aliasing={{0}: (4, {})} | custom-call | tf_op jit(solution)/shard_map/inner/pallas_call | solution.py:421
  73.7 0.0 collective-permute-done.first_ref
  73.7 1.8 %collective-permute-done.1.second_ref = f32[2,72,256]{2,1,0:T(8,128)S(1)} collective-permute-done((f32[2,72,256]{2,1,0:T(8,128)S(1)}, f32[2,72,256]{2,1,0:T(8,128)S(1)}, u32[]{:S(2)}, u32[]{:S(2)}) %collective-permute-start.1) | collective-permute-done | bytes 147488 | tf_op jit(solution)/shard_map/ppermute | solution.py:502
  75.6 1.4 %collective-permute-start.2 = (f32[8,2,256]{2,1,0:T(2,128)S(1)}, f32[8,2,256]{2,1,0:T(2,128)S(1)}, u32[]{:S(2)}, u32[]{:S(2)}) collective-permute-start(f32[8,2,256]{2,1,0:T(2,128)S(1)} %get-tuple-element.16), channel_id=1, source_target_pairs={{0,1},{1,0},{2,3},{3,2},{4,5},{5,4},{6,7},{7,6},{8,9},{9,8},{10,11... | collective-permute-start | bytes 49160 | tf_op jit(solution)/shard_map/ppermute | solution.py:502
  77.0 0.0 collective-permute-start.3
  77.0 0.8 %collective-permute-done.2.near_ref = f32[8,2,256]{2,1,0:T(2,128)S(1)} collective-permute-done((f32[8,2,256]{2,1,0:T(2,128)S(1)}, f32[8,2,256]{2,1,0:T(2,128)S(1)}, u32[]{:S(2)}, u32[]{:S(2)}) %collective-permute-start.2) | collective-permute-done | bytes 16416 | tf_op jit(solution)/shard_map/ppermute | solution.py:502
  77.8 2.3 %collective-permute-done.3.far_ref = f32[8,2,256]{2,1,0:T(2,128)S(1)} collective-permute-done((f32[8,2,256]{2,1,0:T(2,128)S(1)}, f32[8,2,256]{2,1,0:T(2,128)S(1)}, u32[]{:S(2)}, u32[]{:S(2)}) %collective-permute-start.3) | collective-permute-done | bytes 16416 | tf_op jit(solution)/shard_map/ppermute | solution.py:502
  80.1 0.9 %total.1 = f32[8,64,256]{2,1,0:T(8,128)} custom-call(f32[8,72,256]{2,1,0:T(8,128)S(1)} %get-tuple-element.13.cell_ref, f32[2,72,256]{2,1,0:T(8,128)S(1)} %collective-permute-done.first_ref, f32[2,72,256]{2,1,0:T(8,128)S(1)} %collective-permute-done.1.second_ref, f32[8,2,256]{2,1,0:T(2,128)S(1)} %collective-permute-done.2.near_ref, ...), custom_call_target="tpu_custom_call" | custom-call | tf_op jit(solution)/shard_map/total/pallas_call | solution.py:490
  (1 shorter events, 0.0 us)
Async XLA Ops:
  0.6 28.6 %copy-start.1 = (bf16[2,256,256]{2,1,0:T(8,128)(2,1)S(1)}, bf16[2,256,256]{2,1,0:T(8,128)(2,1)}, u32[]{:S(2)}) copy-start(bf16[2,256,256]{2,1,0:T(8,128)(2,1)} %constant.12.clone.slope_ref) | copy-start | bytes 786436
  0.6 28.6 %copy-start.2 = (bf16[2,256,256]{2,1,0:T(8,128)(2,1)S(1)}, bf16[2,256,256]{2,1,0:T(8,128)(2,1)}, u32[]{:S(2)}) copy-start(bf16[2,256,256]{2,1,0:T(8,128)(2,1)} %constant.11.clone.inverse_ref) | copy-start | bytes 786436
  0.7 28.6 %copy-start.3 = (bf16[2,256,256]{2,1,0:T(8,128)(2,1)S(1)}, bf16[2,256,256]{2,1,0:T(8,128)(2,1)}, u32[]{:S(2)}) copy-start(bf16[2,256,256]{2,1,0:T(8,128)(2,1)} %constant.10.clone.table_in.forward_ref) | copy-start | bytes 786436
  0.7 28.6 %copy-start.4 = (bf16[2,256,256]{2,1,0:T(8,128)(2,1)S(1)}, bf16[2,256,256]{2,1,0:T(8,128)(2,1)}, u32[]{:S(2)}) copy-start(bf16[2,256,256]{2,1,0:T(8,128)(2,1)} %constant.14.clone.slope_t_ref) | copy-start | bytes 786436
  0.7 28.6 %copy-start.5 = (bf16[2,256,256]{2,1,0:T(8,128)(2,1)S(1)}, bf16[2,256,256]{2,1,0:T(8,128)(2,1)}, u32[]{:S(2)}) copy-start(bf16[2,256,256]{2,1,0:T(8,128)(2,1)} %constant.13.clone.inverse_t_ref) | copy-start | bytes 786436
  31.6 28.7 %copy-start = (f32[3,8,64,256]{3,2,1,0:T(8,128)S(1)}, f32[3,8,64,256]{3,2,1,0:T(8,128)}, u32[]{:S(2)}) copy-start(f32[3,8,64,256]{3,2,1,0:T(8,128)} %displacement_ref.3) | copy-start | bytes 4718596
  63.5 10.3 %collective-permute-start = (f32[2,72,256]{2,1,0:T(8,128)S(1)}, f32[2,72,256]{2,1,0:T(8,128)S(1)}, u32[]{:S(2)}, u32[]{:S(2)}) collective-permute-start(f32[2,72,256]{2,1,0:T(8,128)S(1)} %get-tuple-element.14), channel_id=1, source_target_pairs={{0,4},{4,0},{8,12},{12,8},{16,20},{20,16},{24,28},{28,24},{32,36},... | collective-permute-start | bytes 442376 | tf_op jit(solution)/shard_map/ppermute | solution.py:502
  64.9 10.7 %collective-permute-start.1 = (f32[2,72,256]{2,1,0:T(8,128)S(1)}, f32[2,72,256]{2,1,0:T(8,128)S(1)}, u32[]{:S(2)}, u32[]{:S(2)}) collective-permute-start(f32[2,72,256]{2,1,0:T(8,128)S(1)} %get-tuple-element.15), channel_id=1, source_target_pairs={{0,124},{4,8},{8,4},{12,16},{16,12},{20,24},{24,20},{28,32},{32,28... | collective-permute-start | bytes 442376 | tf_op jit(solution)/shard_map/ppermute | solution.py:502
  75.6 2.2 %collective-permute-start.2 = (f32[8,2,256]{2,1,0:T(2,128)S(1)}, f32[8,2,256]{2,1,0:T(2,128)S(1)}, u32[]{:S(2)}, u32[]{:S(2)}) collective-permute-start(f32[8,2,256]{2,1,0:T(2,128)S(1)} %get-tuple-element.16), channel_id=1, source_target_pairs={{0,1},{1,0},{2,3},{3,2},{4,5},{5,4},{6,7},{7,6},{8,9},{9,8},{10,11... | collective-permute-start | bytes 49160 | tf_op jit(solution)/shard_map/ppermute | solution.py:502
  77.0 3.2 %collective-permute-start.3 = (f32[8,2,256]{2,1,0:T(2,128)S(1)}, f32[8,2,256]{2,1,0:T(2,128)S(1)}, u32[]{:S(2)}, u32[]{:S(2)}) collective-permute-start(f32[8,2,256]{2,1,0:T(2,128)S(1)} %get-tuple-element.17), channel_id=1, source_target_pairs={{0,3},{1,2},{2,1},{3,0},{4,7},{5,6},{6,5},{7,4},{8,11},{9,10},{10,... | collective-permute-start | bytes 49160 | tf_op jit(solution)/shard_map/ppermute | solution.py:502

commit v4 on v3

--- a/solution.py
+++ b/solution.py
@@ -212,7 +212,6 @@
 
 PAD = 8
 HELD = DEPTH + 2 * PAD
-EDGE_ROWS = (0, 1, ROWS - 2, ROWS - 1)
 
 
 def tile_weights(moved):
@@ -328,73 +327,63 @@
     return [(held[row], row + 2 - cell) for row in sorted(held) if 0 <= row + 2 - cell < 5]
 
 
-def edges_kernel(
-    in_ref, displacement_ref, inverse_ref, slope_ref,
-    psi_out, weight_ref, second_ref, first_ref,
-    psi_ref, sum_ref, psi_sem,
+VMEM = pl.BlockSpec(memory_space=pltpu.VMEM)
+ANY = pl.BlockSpec(memory_space=pl.ANY)
+
+
+def edge_kernel(
+    far, in_ref, displacement_ref, inverse_ref, slope_ref, *refs,
 ):
+    psi_out, weight_ref, halo_ref, psi_ref, sum_ref, psi_sem = refs[-6:]
     inverse = (inverse_ref[0], inverse_ref[1])
     slope = (slope_ref[0], slope_ref[1])
+    even = lax.axis_index("gy") % 2 == 0
+    low = even if far else jnp.logical_not(even)
+    row = jnp.where(low, 0, ROWS - 2)
+    row_pair(row, (0, 1), in_ref, displacement_ref, inverse, slope, psi_ref, weight_ref)
     copies = []
-    for pair, row in enumerate((0, ROWS - 2)):
-        slots = (2 * pair, 2 * pair + 1)
-        row_pair(row, slots, in_ref, displacement_ref, inverse, slope, psi_ref, weight_ref)
-        for part, slot in enumerate(slots):
-            copy = pltpu.make_async_copy(
-                psi_ref.at[slot], psi_out.at[:, row + part], psi_sem.at[slot]
-            )
-            copy.start()
-            copies.append(copy)
-    held = {row: (weight_ref, slot) for slot, row in enumerate(EDGE_ROWS)}
-
-    def cells(before_ref, after_ref):
-        jobs = [(reach(index - 2, held), before_ref, index) for index in range(2)]
-        jobs += [(reach(ROWS + index, held), after_ref, index) for index in range(2)]
-        collect(sum_ref, jobs)
-
-    odd = lax.axis_index("gy") % 2
-
-    @pl.when(odd == 0)
+    for slot in range(2):
+        copy = pltpu.make_async_copy(psi_ref.at[slot], psi_out.at[:, row + slot], psi_sem.at[slot])
+        copy.start()
+        copies.append(copy)
+
+    @pl.when(low)
     def _():
-        cells(second_ref, first_ref)
-
-    @pl.when(odd != 0)
+        held = {0: (weight_ref, 0), 1: (weight_ref, 1)}
+        collect(sum_ref, [(reach(index - 2, held), halo_ref, index) for index in range(2)])
+
+    @pl.when(jnp.logical_not(low))
     def _():
-        cells(first_ref, second_ref)
+        held = {ROWS - 2: (weight_ref, 0), ROWS - 1: (weight_ref, 1)}
+        collect(sum_ref, [(reach(ROWS + index, held), halo_ref, index) for index in range(2)])
 
     for copy in copies:
         copy.wait()
 
 
-VMEM = pl.BlockSpec(memory_space=pltpu.VMEM)
-SMEM = pl.BlockSpec(memory_space=pltpu.SMEM)
-ANY = pl.BlockSpec(memory_space=pl.ANY)
-
-
-def edges(values, displacement, tables):
-    halo = jax.ShapeDtypeStruct((2, DEPTH + PAD, N), f32)
+def edge(far, values, displacement, tables, *psi):
     return pl.pallas_call(
-        edges_kernel,
-        in_specs=[VMEM] * 4,
-        out_specs=[ANY, VMEM, VMEM, VMEM],
+        functools.partial(edge_kernel, far),
+        in_specs=[VMEM] * 4 + [ANY] * len(psi),
+        out_specs=[ANY, VMEM, VMEM],
         out_shape=[
             jax.ShapeDtypeStruct((3, ROWS, DEPTH, N), f32),
-            jax.ShapeDtypeStruct((4, 15, 2, DEPTH + PAD, 128), f32),
-            halo,
-            halo,
+            jax.ShapeDtypeStruct((2, 15, 2, DEPTH + PAD, 128), f32),
+            jax.ShapeDtypeStruct((2, DEPTH + PAD, N), f32),
         ],
         scratch_shapes=[
-            pltpu.VMEM((4, 3, DEPTH, N), f32),
+            pltpu.VMEM((2, 3, DEPTH, N), f32),
             pltpu.VMEM((2, 5, 5, HELD + PAD, 128), f32),
-            pltpu.SemaphoreType.DMA((4,)),
+            pltpu.SemaphoreType.DMA((2,)),
         ],
+        input_output_aliases={4: 0} if psi else {},
         compiler_params=pltpu.CompilerParams(vmem_limit_bytes=16 << 20),
-        name="edges",
-    )(values, displacement, *tables)
+        name="far_edge" if far else "near_edge",
+    )(values, displacement, *tables, *psi)
 
 
 def inner_kernel(
-    in_ref, displacement_ref, inverse_ref, slope_ref, psi_in, edge_ref,
+    in_ref, displacement_ref, inverse_ref, slope_ref, psi_in, far_ref, near_ref,
     psi_out, out_ref,
     psi_ref, weight_ref, sum_ref, psi_sem,
 ):
@@ -410,17 +399,32 @@
             )
             copy.start()
             copies.append(copy)
-    held = {row: (edge_ref, slot) for slot, row in enumerate(EDGE_ROWS)}
-    held.update({row: (weight_ref, row - 2) for row in range(2, ROWS - 2)})
-    collect(sum_ref, [(reach(row, held), out_ref, row) for row in range(ROWS)])
+
+    def cells(low_ref, high_ref):
+        held = {row: (weight_ref, row - 2) for row in range(2, ROWS - 2)}
+        for slot in range(2):
+            held[slot] = (low_ref, slot)
+            held[ROWS - 2 + slot] = (high_ref, slot)
+        collect(sum_ref, [(reach(row, held), out_ref, row) for row in range(ROWS)])
+
+    even = lax.axis_index("gy") % 2 == 0
+
+    @pl.when(even)
+    def _():
+        cells(far_ref, near_ref)
+
+    @pl.when(jnp.logical_not(even))
+    def _():
+        cells(near_ref, far_ref)
+
     for copy in copies:
         copy.wait()
 
 
-def inner(values, displacement, tables, psi, weights):
+def inner(values, displacement, tables, psi, far, near):
     return pl.pallas_call(
         inner_kernel,
-        in_specs=[VMEM] * 4 + [ANY, VMEM],
+        in_specs=[VMEM] * 4 + [ANY, VMEM, VMEM],
         out_specs=[ANY, VMEM],
         out_shape=[
             jax.ShapeDtypeStruct((3, ROWS, DEPTH, N), f32),
@@ -435,7 +439,7 @@
         input_output_aliases={4: 0},
         compiler_params=pltpu.CompilerParams(vmem_limit_bytes=20 << 20),
         name="inner",
-    )(values, displacement, *tables, psi, weights)
+    )(values, displacement, *tables, psi, far, near)
 
 
 def ordered(axis, first, second):
@@ -518,10 +522,11 @@
     returned = lax.all_to_all(returned, both, split_axis=0, concat_axis=0, tiled=True)
     returned = returned.reshape(HALF * 3 * ROWS, 128)
     tables = tables[1:3]
-    psi, weights, second, first = edges(returned, displacement, tables)
+    psi, far_weights, second = edge(True, returned, displacement, tables)
     second = swap(second, "gy", 1)
+    psi, near_weights, first = edge(False, returned, displacement, tables, psi)
     first = swap(first, "gy", 0)
-    psi, cells = inner(returned, displacement, tables, psi, weights)
+    psi, cells = inner(returned, displacement, tables, psi, far_weights, near_weights)
     near, far = sides(cells, first, second)
     far = swap(far, "gz", 1)
     near = swap(near, "gz", 0)

time: 81.1 us -> 78.8 us (0.972)
  waiting for transfers between devices: 4.97 us -> 2.56 us
    ppermute x4, waiting for transfers between devices: 4.97 us -> 2.56 us  [swap(): lax.ppermute(value, axis, [(i, (i + (1 if i % 2 == rounds else -1)) % siz...]
    pallas_call x2 -> x3, Pallas kernels: 10.2 us -> 10.5 us  [the longest x1 7.24 us: inner(): pl.pallas_call(inner_kernel, in_specs=[VMEM] * 4 + [ANY, VMEM, VMEM], out...]
  transfers between devices with their start and end apart: 4 -> 4, of which waited for: 3 -> 2; matrix products, arithmetic and copies ran while one was open for 0% -> 0% of each run, Pallas kernels for 9% -> 11%
where the time goes in v4:
time: 78.8 us; the launch traced here: 78.7 us
  blocking collectives  53.6 us (68%)
  Pallas kernels  17.4 us (22%)
  starting transfers between devices  4.32 us (5%)
  waiting for transfers between devices  2.56 us (3%)
    all_to_all x1, blocking collectives, local(): lax.all_to_all(returned, both, split_axis=0, concat_axis=0, tiled=True)  28.7 us
    all_to_all x1, blocking collectives, local(): lax.all_to_all(spectra, both, split_axis=0, concat_axis=0, tiled=True)  24.8 us
    pallas_call x1, Pallas kernels, inner(): pl.pallas_call(inner_kernel, in_specs=[VMEM] * 4 + [ANY, VMEM, VMEM], out...  7.24 us
    ppermute x4, starting transfers between devices, swap(): lax.ppermute(value, axis, [(i, (i + (1 if i % 2 == rounds else -1)) % siz...  4.32 us
    pallas_call x1, Pallas kernels, lines(): pl.pallas_call(lines_kernel, in_specs=[far] * 3, out_specs=pl.BlockSpec(m...  3.71 us
    pallas_call x2, Pallas kernels, edge(): pl.pallas_call(functools.partial(edge_kernel, far), in_specs=[VMEM] * 4 +...  3.28 us
    ppermute x4, waiting for transfers between devices, swap(): lax.ppermute(value, axis, [(i, (i + (1 if i % 2 == rounds else -1)) % siz...  2.56 us
    pallas_call x1, Pallas kernels, planes(): pl.pallas_call(planes_kernel, in_specs=[whole] * 6, out_specs=whole, out_...  2.27 us
  transfers between devices with their start and end apart: 4, of which 2 were waited for; matrix products, arithmetic and copies ran while one was open for 0% of the time, Pallas kernels for 11%

profile of v4, /device:TPU:1, one launch (start us, length us, event | category | flops | bytes accessed | tf_op | source)
XLA Modules:
  0.0 78.7 jit_solution(15159892932012084110)
XLA Ops:
  0.6 0.0 copy-start.1
  0.6 0.0 copy-start.2
  0.7 0.0 copy-start.3
  0.7 0.0 copy-start.4
  0.7 0.0 copy-start.5
  0.7 3.7 %lines.1 = f32[1024,128]{1,0:T(8,128)S(1)} custom-call(bf16[6,8,64,256]{3,2,1,0:T(8,128)(2,1)} %one_in.1, bf16[6,8,64,256]{3,2,1,0:T(8,128)(2,1)} %two_in.1, bf16[2,256,256]{2,1,0:T(8,128)(2,1)} %constant.10.clone.table_in.forward_ref), custom_call_target="tpu_custom_call" | custom-call | tf_op jit(solution)/shard_map/lines/pallas_call | solution.py:132
  4.4 24.8 %all_to_all.10 = f32[128,8,128]{2,1,0:T(8,128)S(1)} all-to-all(f32[128,8,128]{2,1,0:T(8,128)S(1)} %bitcast.8), channel_id=1, replica_groups=mesh['gy'=32,'gz'=4] {'gy','gz'}, dimensions={0} | all-to-all | bytes 1048576 | tf_op jit(solution)/shard_map/all_to_all | solution.py:519
  29.3 0.0 copy-done.1
  29.3 0.0 copy-done.2
  29.3 0.0 copy-done.3
  29.3 0.0 copy-done.4
  29.3 0.0 copy-done.5
  29.3 2.3 %planes.1 = f32[32,4,24,128]{3,2,1,0:T(8,128)S(1)} custom-call(f32[32,4,8,128]{3,2,1,0:T(8,128)S(1)} %bitcast.9, bf16[2,256,256]{2,1,0:T(8,128)(2,1)S(1)} %copy-done.3, bf16[2,256,256]{2,1,0:T(8,128)(2,1)S(1)} %copy-done.2, bf16[2,256,256]{2,1,0:T(8,128)(2,1)S(1)} %copy-done.1, bf16[2,256,256]{2,1,0:T(8,128)(2,1)S(1)} %copy-done.5, ...), custom_call_target="tpu_custom_call" | custom-call | tf_op jit(solution)/shard_map/planes/pallas_call | solution.py:203
  31.6 0.0 copy-start
  31.6 28.7 %all_to_all.11 = f32[128,24,128]{2,1,0:T(8,128)S(1)} all-to-all(f32[128,24,128]{2,1,0:T(8,128)S(1)} %bitcast.7), channel_id=1, replica_groups=mesh['gy'=32,'gz'=4] {'gy','gz'}, dimensions={0} | all-to-all | bytes 3145728 | tf_op jit(solution)/shard_map/all_to_all | solution.py:522
  60.3 0.0 copy-done
  60.3 1.6 %far_edge.1 = (f32[3,8,64,256]{3,2,1,0:T(8,128)}, f32[2,15,2,72,128]{4,3,2,1,0:T(8,128)S(1)}, f32[2,72,256]{2,1,0:T(8,128)S(1)}) custom-call(f32[3072,128]{1,0:T(8,128)S(1)} %bitcast.4, f32[3,8,64,256]{3,2,1,0:T(8,128)S(1)} %copy-done, bf16[2,256,256]{2,1,0:T(8,128)(2,1)S(1)} %copy-done.2, bf16[2,256,256]{2,1,0:T(8,128)(2,1)S(1)} %copy-done.1), custom_call_target="tpu_custom_call" | custom-call | tf_op jit(solution)/shard_map/far_edge/pallas_call | solution.py:365
  62.0 2.3 %collective-permute-start.1 = (f32[2,72,256]{2,1,0:T(8,128)S(1)}, f32[2,72,256]{2,1,0:T(8,128)S(1)}, u32[]{:S(2)}, u32[]{:S(2)}) collective-permute-start(f32[2,72,256]{2,1,0:T(8,128)S(1)} %get-tuple-element.19), channel_id=1, source_target_pairs={{0,124},{4,8},{8,4},{12,16},{16,12},{20,24},{24,20},{28,32},{32,28... | collective-permute-start | bytes 442376 | tf_op jit(solution)/shard_map/ppermute | solution.py:506
  64.3 1.6 %near_edge.1 = (f32[3,8,64,256]{3,2,1,0:T(8,128)}, f32[2,15,2,72,128]{4,3,2,1,0:T(8,128)S(1)}, f32[2,72,256]{2,1,0:T(8,128)S(1)}) custom-call(f32[3072,128]{1,0:T(8,128)S(1)} %bitcast.5, f32[3,8,64,256]{3,2,1,0:T(8,128)S(1)} %copy-done, bf16[2,256,256]{2,1,0:T(8,128)(2,1)S(1)} %copy-done.2, ...), custom_call_target="tpu_custom_call", output_to_operand_aliasing={{0}: (4, {})} | custom-call | tf_op jit(solution)/shard_map/near_edge/pallas_call | solution.py:365
  65.9 0.1 collective-permute-start
  66.0 7.2 %inner.1 = (f32[3,8,64,256]{3,2,1,0:T(8,128)}, f32[8,72,256]{2,1,0:T(8,128)S(1)}) custom-call(f32[3072,128]{1,0:T(8,128)S(1)} %bitcast.6, f32[3,8,64,256]{3,2,1,0:T(8,128)S(1)} %copy-done, bf16[2,256,256]{2,1,0:T(8,128)(2,1)S(1)} %copy-done.2, bf16[2,256,256]{2,1,0:T(8,128)(2,1)S(1)} %copy-done.1, ...), custom_call_target="tpu_custom_call", output_to_operand_aliasing={{0}: (4, {})} | custom-call | tf_op jit(solution)/shard_map/inner/pallas_call | solution.py:425
  73.2 0.0 collective-permute-done.1.second_ref
  73.2 0.0 collective-permute-done.first_ref
  73.3 1.3 %collective-permute-start.2 = (f32[8,2,256]{2,1,0:T(2,128)S(1)}, f32[8,2,256]{2,1,0:T(2,128)S(1)}, u32[]{:S(2)}, u32[]{:S(2)}) collective-permute-start(f32[8,2,256]{2,1,0:T(2,128)S(1)} %get-tuple-element.20), channel_id=1, source_target_pairs={{0,1},{1,0},{2,3},{3,2},{4,5},{5,4},{6,7},{7,6},{8,9},{9,8},{10,11... | collective-permute-start | bytes 49160 | tf_op jit(solution)/shard_map/ppermute | solution.py:506
  74.6 0.6 collective-permute-start.3
  75.2 0.2 collective-permute-done.2.near_ref
  75.5 2.3 %collective-permute-done.3.far_ref = f32[8,2,256]{2,1,0:T(2,128)S(1)} collective-permute-done((f32[8,2,256]{2,1,0:T(2,128)S(1)}, f32[8,2,256]{2,1,0:T(2,128)S(1)}, u32[]{:S(2)}, u32[]{:S(2)}) %collective-permute-start.3) | collective-permute-done | bytes 16416 | tf_op jit(solution)/shard_map/ppermute | solution.py:506
  77.8 0.9 %total.1 = f32[8,64,256]{2,1,0:T(8,128)} custom-call(f32[8,72,256]{2,1,0:T(8,128)S(1)} %get-tuple-element.17.cell_ref, f32[2,72,256]{2,1,0:T(8,128)S(1)} %collective-permute-done.first_ref, f32[2,72,256]{2,1,0:T(8,128)S(1)} %collective-permute-done.1.second_ref, f32[8,2,256]{2,1,0:T(2,128)S(1)} %collective-permute-done.2.near_ref, ...), custom_call_target="tpu_custom_call" | custom-call | tf_op jit(solution)/shard_map/total/pallas_call | solution.py:494
  (1 shorter events, 0.0 us)
Async XLA Ops:
  0.6 28.6 %copy-start.1 = (bf16[2,256,256]{2,1,0:T(8,128)(2,1)S(1)}, bf16[2,256,256]{2,1,0:T(8,128)(2,1)}, u32[]{:S(2)}) copy-start(bf16[2,256,256]{2,1,0:T(8,128)(2,1)} %constant.12.clone.slope_ref) | copy-start | bytes 786436
  0.6 28.6 %copy-start.2 = (bf16[2,256,256]{2,1,0:T(8,128)(2,1)S(1)}, bf16[2,256,256]{2,1,0:T(8,128)(2,1)}, u32[]{:S(2)}) copy-start(bf16[2,256,256]{2,1,0:T(8,128)(2,1)} %constant.11.clone.inverse_ref) | copy-start | bytes 786436
  0.7 28.6 %copy-start.3 = (bf16[2,256,256]{2,1,0:T(8,128)(2,1)S(1)}, bf16[2,256,256]{2,1,0:T(8,128)(2,1)}, u32[]{:S(2)}) copy-start(bf16[2,256,256]{2,1,0:T(8,128)(2,1)} %constant.10.clone.table_in.forward_ref) | copy-start | bytes 786436
  0.7 28.6 %copy-start.4 = (bf16[2,256,256]{2,1,0:T(8,128)(2,1)S(1)}, bf16[2,256,256]{2,1,0:T(8,128)(2,1)}, u32[]{:S(2)}) copy-start(bf16[2,256,256]{2,1,0:T(8,128)(2,1)} %constant.14.clone.slope_t_ref) | copy-start | bytes 786436
  0.7 28.6 %copy-start.5 = (bf16[2,256,256]{2,1,0:T(8,128)(2,1)S(1)}, bf16[2,256,256]{2,1,0:T(8,128)(2,1)}, u32[]{:S(2)}) copy-start(bf16[2,256,256]{2,1,0:T(8,128)(2,1)} %constant.13.clone.inverse_t_ref) | copy-start | bytes 786436
  31.6 28.7 %copy-start = (f32[3,8,64,256]{3,2,1,0:T(8,128)S(1)}, f32[3,8,64,256]{3,2,1,0:T(8,128)}, u32[]{:S(2)}) copy-start(f32[3,8,64,256]{3,2,1,0:T(8,128)} %displacement_ref.5) | copy-start | bytes 4718596
  62.0 11.3 %collective-permute-start.1 = (f32[2,72,256]{2,1,0:T(8,128)S(1)}, f32[2,72,256]{2,1,0:T(8,128)S(1)}, u32[]{:S(2)}, u32[]{:S(2)}) collective-permute-start(f32[2,72,256]{2,1,0:T(8,128)S(1)} %get-tuple-element.19), channel_id=1, source_target_pairs={{0,124},{4,8},{8,4},{12,16},{16,12},{20,24},{24,20},{28,32},{32,28... | collective-permute-start | bytes 442376 | tf_op jit(solution)/shard_map/ppermute | solution.py:506
  65.9 7.3 %collective-permute-start = (f32[2,72,256]{2,1,0:T(8,128)S(1)}, f32[2,72,256]{2,1,0:T(8,128)S(1)}, u32[]{:S(2)}, u32[]{:S(2)}) collective-permute-start(f32[2,72,256]{2,1,0:T(8,128)S(1)} %get-tuple-element.18), channel_id=1, source_target_pairs={{0,4},{4,0},{8,12},{12,8},{16,20},{20,16},{24,28},{28,24},{32,36},... | collective-permute-start | bytes 442376 | tf_op jit(solution)/shard_map/ppermute | solution.py:506
  73.3 2.2 %collective-permute-start.2 = (f32[8,2,256]{2,1,0:T(2,128)S(1)}, f32[8,2,256]{2,1,0:T(2,128)S(1)}, u32[]{:S(2)}, u32[]{:S(2)}) collective-permute-start(f32[8,2,256]{2,1,0:T(2,128)S(1)} %get-tuple-element.20), channel_id=1, source_target_pairs={{0,1},{1,0},{2,3},{3,2},{4,5},{5,4},{6,7},{7,6},{8,9},{9,8},{10,11... | collective-permute-start | bytes 49160 | tf_op jit(solution)/shard_map/ppermute | solution.py:506
  74.6 3.2 %collective-permute-start.3 = (f32[8,2,256]{2,1,0:T(2,128)S(1)}, f32[8,2,256]{2,1,0:T(2,128)S(1)}, u32[]{:S(2)}, u32[]{:S(2)}) collective-permute-start(f32[8,2,256]{2,1,0:T(2,128)S(1)} %get-tuple-element.21), channel_id=1, source_target_pairs={{0,3},{1,2},{2,1},{3,0},{4,7},{5,6},{6,5},{7,4},{8,11},{9,10},{10,... | collective-permute-start | bytes 49160 | tf_op jit(solution)/shard_map/ppermute | solution.py:506
